TPU v7x, 256 devices: a whole 4x4x8 slice. The times are simulated.
256 devices in a mesh: bx: 32 (over z, y), by: 8 (over x, core).
Axes of the slice: x: 4, y: 4, z: 8, core: 2. Of those that a mesh axis runs over, the one named last changes fastest.
Arguments:
- source: bfloat16 [32, 8, 2, 128, 1024], P('bx', 'by'), may hold values from -6 to 6
- start_tick: int32 [32, 8], P('bx', 'by'), may hold values from 0 to 3, as said below
- op_x: bfloat16 [32, 8, 2, 1024, 1024], P('bx', 'by'), may hold values from -0.09375 to 0.09375
- op_y: bfloat16 [32, 8, 2, 1024, 1024], P('bx', 'by'), may hold values from -0.09375 to 0.09375
Outputs:
- upgoing: float32 [8, 128, 2, 32, 1024], P('by', 'bx')
Inputs may be any that keep to these rules, and one draw needn't show every extreme that they name: `start_tick`: both 0 and 3 occur in every draw.
All inputs are finite; a program needn't handle non-finite values.
Results may differ from a plain program's by a relative error of at most 0.012.
Values may be sent and summed in bfloat16 or wider, within the bound.
No kernel may reach another device: no remote copies, remote signals or barrier semaphores. Data moves between devices by JAX's collectives and lax.ppermute only.
A program may use at most 64 MiB of HBM per device.

v0:
```python
import math

import jax
import jax.numpy as jnp
from jax import lax
from jax.sharding import PartitionSpec as P

F = 1024
TICKS = 4


def passed_along(value, axis, by):
    peers = lax.axis_size(axis)
    pairs = [(i, i + by) for i in range(peers) if 0 <= i + by < peers]
    return lax.ppermute(value, axis, pairs)


def with_halo(block, sides, width):
    for axis, dim in sides:
        count = lax.axis_size(axis)
        forward = [(i, i + 1) for i in range(count - 1)]
        backward = [(target, source) for source, target in forward]
        low = lax.ppermute(
            lax.slice_in_dim(block, block.shape[dim] - width, None, axis=dim), axis, forward
        )
        high = lax.ppermute(lax.slice_in_dim(block, 0, width, axis=dim), axis, backward)
        block = jnp.concatenate([low, block, high], axis=dim)
    return block


def dft_tables(length):
    indices = jnp.arange(length, dtype=jnp.int32)
    products = indices[:, None] * indices[None, :] % length
    angles = products.astype(jnp.float32) * (2.0 * math.pi / length)
    return (jnp.cos(angles).astype(jnp.bfloat16), jnp.sin(angles).astype(jnp.bfloat16))


def complex_apply(traces, operator):
    shot_count = traces.shape[1]
    stacked = traces.reshape(2 * shot_count, traces.shape[2])
    with_real = jnp.dot(stacked, operator[0], preferred_element_type=jnp.float32)
    with_imag = jnp.dot(stacked, operator[1], preferred_element_type=jnp.float32)
    real_out = with_real[:shot_count] - with_imag[shot_count:]
    imag_out = with_imag[:shot_count] + with_real[shot_count:]
    return jnp.stack([real_out, imag_out])


def line_spectrum(values, cos_line, sin_line):
    old_shape = values.shape
    flattened = values.reshape(2, -1, old_shape[-1])
    row_count = flattened.shape[1]
    stacked = flattened.reshape(2 * row_count, old_shape[-1])
    cosine_part = jnp.dot(stacked, cos_line, preferred_element_type=jnp.float32)
    sine_part = jnp.dot(stacked, sin_line, preferred_element_type=jnp.float32)
    real_out = cosine_part[:row_count] + sine_part[row_count:]
    imag_out = cosine_part[row_count:] - sine_part[:row_count]
    return jnp.stack([real_out, imag_out]).reshape(old_shape).astype(jnp.bfloat16)


def shards(source, start_tick, op_x, op_y):
    local_source = source[0, 0].astype(jnp.float32)
    operator_x = op_x[0, 0]
    operator_y = op_y[0, 0]
    first_tick = start_tick[0, 0]
    shot_count = local_source.shape[1]
    east_out = None
    north_out = None
    for tick in range(TICKS):
        active = (first_tick <= tick).astype(jnp.float32)
        if tick == 0:
            incident = (active * local_source).astype(jnp.bfloat16)
        else:
            from_west = passed_along(east_out, "bx", 1)
            from_south = passed_along(north_out, "by", 1)
            incident = (
                from_west.astype(jnp.float32)
                + from_south.astype(jnp.float32)
                + active * local_source
            ).astype(jnp.bfloat16)
        east_out = complex_apply(incident, operator_x).astype(jnp.bfloat16)
        north_out = complex_apply(incident, operator_y).astype(jnp.bfloat16)
    stacked = jnp.stack([east_out, north_out]).reshape((1, 1, 2) + east_out.shape)
    padded = with_halo(stacked, (("bx", 0), ("by", 1)), 1)
    from_west = padded[0, 1, 0]
    from_east = padded[2, 1, 0]
    from_south = padded[1, 0, 1]
    from_north = padded[1, 2, 1]
    mismatch = (
        from_west.astype(jnp.float32)
        + from_south.astype(jnp.float32)
        - from_east.astype(jnp.float32)
        - from_north.astype(jnp.float32)
    ).astype(jnp.bfloat16)
    reflected = complex_apply(mismatch, operator_x).astype(jnp.bfloat16)
    cos_line, sin_line = dft_tables(F)
    pieces = lax.axis_size("bx")
    owned = shot_count // pieces
    arranged = reflected.reshape(2, pieces, owned, 1, F)
    regrouped = line_spectrum(
        lax.all_to_all(arranged, "bx", split_axis=1, concat_axis=3, tiled=True), cos_line, sin_line
    )
    spectrum = regrouped.reshape(2, owned, pieces, F)
    cos_grid, sin_grid = dft_tables(pieces)
    out_real = jnp.einsum(
        "sik,iq->sqk", spectrum[0], cos_grid, preferred_element_type=jnp.float32
    ) + jnp.einsum("sik,iq->sqk", spectrum[1], sin_grid, preferred_element_type=jnp.float32)
    out_imag = jnp.einsum(
        "sik,iq->sqk", spectrum[1], cos_grid, preferred_element_type=jnp.float32
    ) - jnp.einsum("sik,iq->sqk", spectrum[0], sin_grid, preferred_element_type=jnp.float32)
    wave_index = jnp.arange(pieces, dtype=jnp.int32)
    signed = jnp.where(wave_index < pieces // 2, wave_index, wave_index - pieces).astype(
        jnp.float32
    )
    weights = 0.5 * (1.0 + signed / jnp.sqrt(signed * signed + 1.0))
    upgoing = jnp.stack([out_real, out_imag], axis=1) * weights[None, None, :, None]
    return upgoing.reshape((1,) + upgoing.shape)


def solution(mesh):
    placed = (
        P("bx", "by", None, None, None),
        P("bx", "by"),
        P("bx", "by", None, None, None),
        P("bx", "by", None, None, None),
    )
    return jax.shard_map(
        shards,
        mesh=mesh,
        in_specs=placed,
        out_specs=P("by", "bx", None, None, None),
        check_vma=False,
    )
```

profile of v0, /device:TPU:3, one launch (start us, length us, event | category | flops | bytes accessed | tf_op | source)
XLA Modules:
  0.0 209.4 jit_solution(9184586754677524131)
XLA Ops:
  0.8 1.3 fusion.66
  2.1 2.3 %fusion.32 = f32[256,1024]{1,0:T(8,128)S(1)} fusion(bf16[256,1024]{1,0:T(8,128)(2,1)S(1)} %bitcast.172, bf16[1,1,2,1024,1024]{4,3,2,1,0:T(8,128)(2,1)} %param.6), kind=kOutput, calls=%fused_computation.38 | convolution fusion | flops 536870912 | bytes 3670016 | tf_op jit(solution)/shard_map/dot_general | solution.py:42
  4.4 0.7 fusion.42
  5.2 0.2 fusion.96
  5.4 3.4 %collective-permute-start = (bf16[2,128,1024]{2,1,0:T(8,128)(2,1)S(1)}, bf16[2,128,1024]{2,1,0:T(8,128)(2,1)S(1)}, u32[]{:S(2)}, u32[]{:S(2)}) collective-permute-start(bf16[2,128,1024]{2,1,0:T(8,128)(2,1)S(1)} %pad_maximum_fusion.1), channel_id=1, source_target_pairs={{0,8},{8,16},{16,24},{24,32},{32,40},{40,48},{48,56},{56,64},{64,7... | collective-permute-start | bytes 1572872 | tf_op jit(solution)/shard_map/ppermute | solution.py:15
  8.8 0.7 fusion.14
  9.6 0.7 fusion.22
  10.3 0.2 fusion.98
  10.6 4.0 %collective-permute-start.1 = (bf16[2,128,1024]{2,1,0:T(8,128)(2,1)S(1)}, bf16[2,128,1024]{2,1,0:T(8,128)(2,1)S(1)}, u32[]{:S(2)}, u32[]{:S(2)}) collective-permute-start(bf16[2,128,1024]{2,1,0:T(8,128)(2,1)S(1)} %pad_maximum_fusion.2), channel_id=1, source_target_pairs={{0,1},{1,2},{2,3},{3,4},{4,5},{5,6},{6,7},{8,9},{9,10},{10,11},{11... | collective-permute-start | bytes 1572872 | tf_op jit(solution)/shard_map/ppermute | solution.py:15
  14.5 4.8 %collective-permute-done = bf16[2,128,1024]{2,1,0:T(8,128)(2,1)S(1)} collective-permute-done((bf16[2,128,1024]{2,1,0:T(8,128)(2,1)S(1)}, bf16[2,128,1024]{2,1,0:T(8,128)(2,1)S(1)}, u32[]{:S(2)}, u32[]{:S(2)}) %collective-permute-start) | collective-permute-done | bytes 524320 | tf_op jit(solution)/shard_map/ppermute | solution.py:15
  19.4 1.3 collective-permute-done.1
  20.6 0.3 fusion.69
  20.9 0.7 fusion.30
  21.6 0.7 fusion.40
  22.3 0.7 fusion.12
  23.1 0.7 fusion.20
  23.8 0.2 fusion.100
  24.1 3.2 %collective-permute-start.2 = (bf16[2,128,1024]{2,1,0:T(8,128)(2,1)S(1)}, bf16[2,128,1024]{2,1,0:T(8,128)(2,1)S(1)}, u32[]{:S(2)}, u32[]{:S(2)}) collective-permute-start(bf16[2,128,1024]{2,1,0:T(8,128)(2,1)S(1)} %pad_maximum_fusion.3), channel_id=1, source_target_pairs={{0,8},{8,16},{16,24},{24,32},{32,40},{40,48},{48,56},{56,64},{64,7... | collective-permute-start | bytes 1572872 | tf_op jit(solution)/shard_map/ppermute | solution.py:15
  27.3 0.2 fusion.102
  27.5 4.7 %collective-permute-start.3 = (bf16[2,128,1024]{2,1,0:T(8,128)(2,1)S(1)}, bf16[2,128,1024]{2,1,0:T(8,128)(2,1)S(1)}, u32[]{:S(2)}, u32[]{:S(2)}) collective-permute-start(bf16[2,128,1024]{2,1,0:T(8,128)(2,1)S(1)} %pad_maximum_fusion.4), channel_id=1, source_target_pairs={{0,1},{1,2},{2,3},{3,4},{4,5},{5,6},{6,7},{8,9},{9,10},{10,11},{11... | collective-permute-start | bytes 1572872 | tf_op jit(solution)/shard_map/ppermute | solution.py:15
  32.2 4.9 %collective-permute-done.2 = bf16[2,128,1024]{2,1,0:T(8,128)(2,1)S(1)} collective-permute-done((bf16[2,128,1024]{2,1,0:T(8,128)(2,1)S(1)}, bf16[2,128,1024]{2,1,0:T(8,128)(2,1)S(1)}, u32[]{:S(2)}, u32[]{:S(2)}) %collective-permute-start.2) | collective-permute-done | bytes 524320 | tf_op jit(solution)/shard_map/ppermute | solution.py:15
  37.1 1.2 collective-permute-done.3
  38.3 0.3 fusion.72
  38.6 0.7 fusion.28
  39.3 0.7 fusion.38
  40.0 0.7 fusion.10
  40.8 0.7 fusion.18
  41.5 0.2 fusion.104
  41.8 3.0 %collective-permute-start.4 = (bf16[2,128,1024]{2,1,0:T(8,128)(2,1)S(1)}, bf16[2,128,1024]{2,1,0:T(8,128)(2,1)S(1)}, u32[]{:S(2)}, u32[]{:S(2)}) collective-permute-start(bf16[2,128,1024]{2,1,0:T(8,128)(2,1)S(1)} %pad_maximum_fusion.5), channel_id=1, source_target_pairs={{0,8},{8,16},{16,24},{24,32},{32,40},{40,48},{48,56},{56,64},{64,7... | collective-permute-start | bytes 1572872 | tf_op jit(solution)/shard_map/ppermute | solution.py:15
  44.8 0.2 fusion.106
  45.1 5.3 %collective-permute-start.5 = (bf16[2,128,1024]{2,1,0:T(8,128)(2,1)S(1)}, bf16[2,128,1024]{2,1,0:T(8,128)(2,1)S(1)}, u32[]{:S(2)}, u32[]{:S(2)}) collective-permute-start(bf16[2,128,1024]{2,1,0:T(8,128)(2,1)S(1)} %pad_maximum_fusion.6), channel_id=1, source_target_pairs={{0,1},{1,2},{2,3},{3,4},{4,5},{5,6},{6,7},{8,9},{9,10},{10,11},{11... | collective-permute-start | bytes 1572872 | tf_op jit(solution)/shard_map/ppermute | solution.py:15
  50.4 3.5 %collective-permute-done.4 = bf16[2,128,1024]{2,1,0:T(8,128)(2,1)S(1)} collective-permute-done((bf16[2,128,1024]{2,1,0:T(8,128)(2,1)S(1)}, bf16[2,128,1024]{2,1,0:T(8,128)(2,1)S(1)}, u32[]{:S(2)}, u32[]{:S(2)}) %collective-permute-start.4) | collective-permute-done | bytes 524320 | tf_op jit(solution)/shard_map/ppermute | solution.py:15
  53.9 2.4 %collective-permute-done.5 = bf16[2,128,1024]{2,1,0:T(8,128)(2,1)S(1)} collective-permute-done((bf16[2,128,1024]{2,1,0:T(8,128)(2,1)S(1)}, bf16[2,128,1024]{2,1,0:T(8,128)(2,1)S(1)}, u32[]{:S(2)}, u32[]{:S(2)}) %collective-permute-start.5) | collective-permute-done | bytes 524320 | tf_op jit(solution)/shard_map/ppermute | solution.py:15
  56.3 0.3 fusion.75
  56.6 0.7 fusion.16
  57.3 0.7 fusion.26
  58.0 0.7 fusion.36
  58.7 0.7 fusion.8
  59.5 0.5 fusion.108
  60.1 3.2 %collective-permute-start.6 = (bf16[1,1,2,2,128,1024]{5,4,3,2,1,0:T(8,128)(2,1)S(1)}, bf16[1,1,2,2,128,1024]{5,4,3,2,1,0:T(8,128)(2,1)S(1)}, u32[]{:S(2)}, u32[]{:S(2)}) collective-permute-start(bf16[1,1,2,2,128,1024]{5,4,3,2,1,0:T(8,128)(2,1)S(1)} %maximum_bitcast_fusion), channel_id=1, source_target_pairs={{0,8},{8,16},{16,24},{24,32},{32,40},{40,48},{48,56},{56,64},{64,7... | collective-permute-start | bytes 3145736 | tf_op jit(solution)/shard_map/ppermute | solution.py:23
  63.3 1.3 collective-permute-start.7
  64.6 19.6 %collective-permute-done.6 = bf16[1,1,2,2,128,1024]{5,4,3,2,1,0:T(8,128)(2,1)S(1)} collective-permute-done((bf16[1,1,2,2,128,1024]{5,4,3,2,1,0:T(8,128)(2,1)S(1)}, bf16[1,1,2,2,128,1024]{5,4,3,2,1,0:T(8,128)(2,1)S(1)}, u32[]{:S(2)}, u32[]{:S(2)}) %collective-permute-start.6) | collective-permute-done | bytes 1048608 | tf_op jit(solution)/shard_map/ppermute | solution.py:23
  84.2 5.5 %collective-permute-done.7 = bf16[1,1,2,2,128,1024]{5,4,3,2,1,0:T(8,128)(2,1)S(1)} collective-permute-done((bf16[1,1,2,2,128,1024]{5,4,3,2,1,0:T(8,128)(2,1)S(1)}, bf16[1,1,2,2,128,1024]{5,4,3,2,1,0:T(8,128)(2,1)S(1)}, u32[]{:S(2)}, u32[]{:S(2)}) %collective-permute-start.7) | collective-permute-done | bytes 1048608 | tf_op jit(solution)/shard_map/ppermute | solution.py:26
  89.7 0.3 pad_maximum_fusion
  90.1 5.0 %collective-permute-start.8 = (bf16[3,1,2,2,128,1024]{5,4,3,2,1,0:T(8,128)(2,1)S(1)}, bf16[3,1,2,2,128,1024]{5,4,3,2,1,0:T(8,128)(2,1)S(1)}, u32[]{:S(2)}, u32[]{:S(2)}) collective-permute-start(bf16[3,1,2,2,128,1024]{5,4,3,2,1,0:T(8,128)(2,1)S(1)} %pad_maximum_fusion), channel_id=1, source_target_pairs={{0,1},{1,2},{2,3},{3,4},{4,5},{5,6},{6,7},{8,9},{9,10},{10,11},{11... | collective-permute-start | bytes 9437192 | tf_op jit(solution)/shard_map/ppermute | solution.py:23
  95.0 1.9 collective-permute-start.9
  97.0 32.3 %collective-permute-done.8 = bf16[3,1,2,2,128,1024]{5,4,3,2,1,0:T(8,128)(2,1)S(1)} collective-permute-done((bf16[3,1,2,2,128,1024]{5,4,3,2,1,0:T(8,128)(2,1)S(1)}, bf16[3,1,2,2,128,1024]{5,4,3,2,1,0:T(8,128)(2,1)S(1)}, u32[]{:S(2)}, u32[]{:S(2)}) %collective-permute-start.8) | collective-permute-done | bytes 3145760 | tf_op jit(solution)/shard_map/ppermute | solution.py:23
  129.2 4.4 %collective-permute-done.9 = bf16[3,1,2,2,128,1024]{5,4,3,2,1,0:T(8,128)(2,1)S(1)} collective-permute-done((bf16[3,1,2,2,128,1024]{5,4,3,2,1,0:T(8,128)(2,1)S(1)}, bf16[3,1,2,2,128,1024]{5,4,3,2,1,0:T(8,128)(2,1)S(1)}, u32[]{:S(2)}, u32[]{:S(2)}) %collective-permute-start.9) | collective-permute-done | bytes 3145760 | tf_op jit(solution)/shard_map/ppermute | solution.py:26
  133.6 0.4 subtract_convert_fusion
  134.0 0.7 fusion.24
  134.7 0.7 fusion.34
  135.4 0.2 fusion.79
  135.8 1.1 pad_maximum_fusion.7
  137.0 20.0 %all-to-all-start = ((bf16[2,32,4,1,1024]{4,2,0,3,1:T(4,128)(2,1)}), bf16[2,32,4,1,1024]{4,2,0,3,1:T(4,128)(2,1)S(1)}, u32[]{:S(2)}, u32[]{:S(2)}) async-start(bf16[2,32,4,1,1024]{4,2,0,3,1:T(4,128)(2,1)} %pad_maximum_fusion.7), calls=%async_computation | async-start | bytes 1048576 | tf_op jit(solution)/shard_map/all_to_all | solution.py:100
  157.0 17.1 %all-to-all-done = bf16[2,32,4,1,1024]{4,2,0,3,1:T(4,128)(2,1)S(1)} async-done(((bf16[2,32,4,1,1024]{4,2,0,3,1:T(4,128)(2,1)}), bf16[2,32,4,1,1024]{4,2,0,3,1:T(4,128)(2,1)S(1)}, u32[]{:S(2)}, u32[]{:S(2)}) %all-to-all-start) | async-done | bytes 524320 | tf_op jit(solution)/shard_map/all_to_all | solution.py:100
  174.0 0.3 copy.11
  174.3 16.1 %fusion.6 = f32[256,1024]{1,0:T(8,128)S(1)} fusion(bf16[256,1024]{1,0:T(8,128)(2,1)S(1)} %bitcast.170), kind=kOutput, calls=%fused_computation.12 | convolution fusion | flops 552599552 | bytes 1572864 | tf_op jit(solution)/shard_map/dot_general | solution.py:53
  190.5 16.3 %fusion.7 = f32[256,1024]{1,0:T(8,128)S(1)} fusion(bf16[256,1024]{1,0:T(8,128)(2,1)S(1)} %bitcast.171), kind=kOutput, calls=%fused_computation.13 | convolution fusion | flops 552599552 | bytes 1572864 | tf_op jit(solution)/shard_map/dot_general | solution.py:54
  206.7 0.2 fusion.77
  206.9 0.3 fusion.124
  207.2 0.3 fusion.122
  207.5 0.3 fusion.55
  207.8 0.3 fusion.54
  208.3 1.1 copy.12
  (17 shorter events, 0.8 us)
Async XLA Ops:
  0.0 4.4 %copy-start.2 = (bf16[1,1,2,1024,1024]{4,3,2,1,0:T(8,128)(2,1)S(1)}, bf16[1,1,2,1024,1024]{4,3,2,1,0:T(8,128)(2,1)}, u32[]{:S(2)}) copy-start(bf16[1,1,2,1024,1024]{4,3,2,1,0:T(8,128)(2,1)} %param.6) | copy-start | bytes 12582916
  4.4 4.4 %copy-start.1 = (bf16[1,1,2,1024,1024]{4,3,2,1,0:T(8,128)(2,1)S(1)}, bf16[1,1,2,1024,1024]{4,3,2,1,0:T(8,128)(2,1)}, u32[]{:S(2)}) copy-start(bf16[1,1,2,1024,1024]{4,3,2,1,0:T(8,128)(2,1)} %param.7) | copy-start | bytes 12582916
  5.4 13.9 %collective-permute-start = (bf16[2,128,1024]{2,1,0:T(8,128)(2,1)S(1)}, bf16[2,128,1024]{2,1,0:T(8,128)(2,1)S(1)}, u32[]{:S(2)}, u32[]{:S(2)}) collective-permute-start(bf16[2,128,1024]{2,1,0:T(8,128)(2,1)S(1)} %pad_maximum_fusion.1), channel_id=1, source_target_pairs={{0,8},{8,16},{16,24},{24,32},{32,40},{40,48},{48,56},{56,64},{64,7... | collective-permute-start | bytes 1572872 | tf_op jit(solution)/shard_map/ppermute | solution.py:15
  9.5 11.1 %copy-start = (bf16[1,1,2,128,1024]{4,3,2,1,0:T(8,128)(2,1)S(1)}, bf16[1,1,2,128,1024]{4,3,2,1,0:T(8,128)(2,1)}, u32[]{:S(2)}) copy-start(bf16[1,1,2,128,1024]{4,3,2,1,0:T(8,128)(2,1)} %param.4) | copy-start | bytes 1572868
  10.6 10.1 %collective-permute-start.1 = (bf16[2,128,1024]{2,1,0:T(8,128)(2,1)S(1)}, bf16[2,128,1024]{2,1,0:T(8,128)(2,1)S(1)}, u32[]{:S(2)}, u32[]{:S(2)}) collective-permute-start(bf16[2,128,1024]{2,1,0:T(8,128)(2,1)S(1)} %pad_maximum_fusion.2), channel_id=1, source_target_pairs={{0,1},{1,2},{2,3},{3,4},{4,5},{5,6},{6,7},{8,9},{9,10},{10,11},{11... | collective-permute-start | bytes 1572872 | tf_op jit(solution)/shard_map/ppermute | solution.py:15
  24.1 13.1 %collective-permute-start.2 = (bf16[2,128,1024]{2,1,0:T(8,128)(2,1)S(1)}, bf16[2,128,1024]{2,1,0:T(8,128)(2,1)S(1)}, u32[]{:S(2)}, u32[]{:S(2)}) collective-permute-start(bf16[2,128,1024]{2,1,0:T(8,128)(2,1)S(1)} %pad_maximum_fusion.3), channel_id=1, source_target_pairs={{0,8},{8,16},{16,24},{24,32},{32,40},{40,48},{48,56},{56,64},{64,7... | collective-permute-start | bytes 1572872 | tf_op jit(solution)/shard_map/ppermute | solution.py:15
  27.5 10.8 %collective-permute-start.3 = (bf16[2,128,1024]{2,1,0:T(8,128)(2,1)S(1)}, bf16[2,128,1024]{2,1,0:T(8,128)(2,1)S(1)}, u32[]{:S(2)}, u32[]{:S(2)}) collective-permute-start(bf16[2,128,1024]{2,1,0:T(8,128)(2,1)S(1)} %pad_maximum_fusion.4), channel_id=1, source_target_pairs={{0,1},{1,2},{2,3},{3,4},{4,5},{5,6},{6,7},{8,9},{9,10},{10,11},{11... | collective-permute-start | bytes 1572872 | tf_op jit(solution)/shard_map/ppermute | solution.py:15
  41.8 12.1 %collective-permute-start.4 = (bf16[2,128,1024]{2,1,0:T(8,128)(2,1)S(1)}, bf16[2,128,1024]{2,1,0:T(8,128)(2,1)S(1)}, u32[]{:S(2)}, u32[]{:S(2)}) collective-permute-start(bf16[2,128,1024]{2,1,0:T(8,128)(2,1)S(1)} %pad_maximum_fusion.5), channel_id=1, source_target_pairs={{0,8},{8,16},{16,24},{24,32},{32,40},{40,48},{48,56},{56,64},{64,7... | collective-permute-start | bytes 1572872 | tf_op jit(solution)/shard_map/ppermute | solution.py:15
  45.1 11.2 %collective-permute-start.5 = (bf16[2,128,1024]{2,1,0:T(8,128)(2,1)S(1)}, bf16[2,128,1024]{2,1,0:T(8,128)(2,1)S(1)}, u32[]{:S(2)}, u32[]{:S(2)}) collective-permute-start(bf16[2,128,1024]{2,1,0:T(8,128)(2,1)S(1)} %pad_maximum_fusion.6), channel_id=1, source_target_pairs={{0,1},{1,2},{2,3},{3,4},{4,5},{5,6},{6,7},{8,9},{9,10},{10,11},{11... | collective-permute-start | bytes 1572872 | tf_op jit(solution)/shard_map/ppermute | solution.py:15
  60.1 24.1 %collective-permute-start.6 = (bf16[1,1,2,2,128,1024]{5,4,3,2,1,0:T(8,128)(2,1)S(1)}, bf16[1,1,2,2,128,1024]{5,4,3,2,1,0:T(8,128)(2,1)S(1)}, u32[]{:S(2)}, u32[]{:S(2)}) collective-permute-start(bf16[1,1,2,2,128,1024]{5,4,3,2,1,0:T(8,128)(2,1)S(1)} %maximum_bitcast_fusion), channel_id=1, source_target_pairs={{0,8},{8,16},{16,24},{24,32},{32,40},{40,48},{48,56},{56,64},{64,7... | collective-permute-start | bytes 3145736 | tf_op jit(solution)/shard_map/ppermute | solution.py:23
  63.3 26.4 %collective-permute-start.7 = (bf16[1,1,2,2,128,1024]{5,4,3,2,1,0:T(8,128)(2,1)S(1)}, bf16[1,1,2,2,128,1024]{5,4,3,2,1,0:T(8,128)(2,1)S(1)}, u32[]{:S(2)}, u32[]{:S(2)}) collective-permute-start(bf16[1,1,2,2,128,1024]{5,4,3,2,1,0:T(8,128)(2,1)S(1)} %maximum_bitcast_fusion), channel_id=1, source_target_pairs={{8,0},{16,8},{24,16},{32,24},{40,32},{48,40},{56,48},{64,56},{72,6... | collective-permute-start | bytes 3145736 | tf_op jit(solution)/shard_map/ppermute | solution.py:26
  90.1 39.2 %collective-permute-start.8 = (bf16[3,1,2,2,128,1024]{5,4,3,2,1,0:T(8,128)(2,1)S(1)}, bf16[3,1,2,2,128,1024]{5,4,3,2,1,0:T(8,128)(2,1)S(1)}, u32[]{:S(2)}, u32[]{:S(2)}) collective-permute-start(bf16[3,1,2,2,128,1024]{5,4,3,2,1,0:T(8,128)(2,1)S(1)} %pad_maximum_fusion), channel_id=1, source_target_pairs={{0,1},{1,2},{2,3},{3,4},{4,5},{5,6},{6,7},{8,9},{9,10},{10,11},{11... | collective-permute-start | bytes 9437192 | tf_op jit(solution)/shard_map/ppermute | solution.py:23
  95.0 38.6 %collective-permute-start.9 = (bf16[3,1,2,2,128,1024]{5,4,3,2,1,0:T(8,128)(2,1)S(1)}, bf16[3,1,2,2,128,1024]{5,4,3,2,1,0:T(8,128)(2,1)S(1)}, u32[]{:S(2)}, u32[]{:S(2)}) collective-permute-start(bf16[3,1,2,2,128,1024]{5,4,3,2,1,0:T(8,128)(2,1)S(1)} %pad_maximum_fusion), channel_id=1, source_target_pairs={{1,0},{2,1},{3,2},{4,3},{5,4},{6,5},{7,6},{9,8},{10,9},{11,10},{12... | collective-permute-start | bytes 9437192 | tf_op jit(solution)/shard_map/ppermute | solution.py:26
  137.0 37.1 %all-to-all-start = ((bf16[2,32,4,1,1024]{4,2,0,3,1:T(4,128)(2,1)}), bf16[2,32,4,1,1024]{4,2,0,3,1:T(4,128)(2,1)S(1)}, u32[]{:S(2)}, u32[]{:S(2)}) async-start(bf16[2,32,4,1,1024]{4,2,0,3,1:T(4,128)(2,1)} %pad_maximum_fusion.7), calls=%async_computation | async-start | bytes 1048576 | tf_op jit(solution)/shard_map/all_to_all | solution.py:100
where the time goes:
time: 210 us; the launch traced here: 209 us
  waiting for transfers between devices  96.9 us (46%)
  starting transfers between devices  54.9 us (26%)
  matrix products  47.9 us (23%)
  other arithmetic  6.75 us (3%)
    ppermute x2, waiting for transfers between devices, with_halo(): lax.ppermute(lax.slice_in_dim(block, block.shape[dim] - width, None, axis...  51.9 us
    ppermute x6, starting transfers between devices, passed_along(): return lax.ppermute(value, axis, pairs)  23.5 us
    all_to_all x1, starting transfers between devices, shards(): lax.all_to_all(arranged, 'bx', split_axis=1, concat_axis=3, tiled=True)  20 us
    ppermute x6, waiting for transfers between devices, passed_along(): return lax.ppermute(value, axis, pairs)  18.1 us
    all_to_all x1, waiting for transfers between devices, shards(): lax.all_to_all(arranged, 'bx', split_axis=1, concat_axis=3, tiled=True)  17.1 us
    dot_general x1, matrix products, line_spectrum(): sine_part = jnp.dot(stacked, sin_line, preferred_element_type=jnp.float32)  16.3 us
    dot_general x1, matrix products, line_spectrum(): cosine_part = jnp.dot(stacked, cos_line, preferred_element_type=jnp.float32)  16.1 us
    ppermute x2, waiting for transfers between devices, with_halo(): lax.ppermute(lax.slice_in_dim(block, 0, width, axis=dim), axis, backward)  9.87 us
  transfers between devices with their start and end apart: 11, of which 11 were waited for; matrix products, arithmetic and copies ran while one was open for 1% of the time, Pallas kernels for 0%

commit v1 on v0

v1 whole, which is shorter than its diff:
```python
import math

import jax
import jax.numpy as jnp
import numpy as np
from jax import lax
from jax.sharding import PartitionSpec as P

F = 1024
TICKS = 4
SHOTS = 128


def shift(value, axis, by):
    n = lax.axis_size(axis)
    return lax.ppermute(value, axis, [(i, (i + by) % n) for i in range(n)])


def paired(block):
    re, im = block[0], block[1]
    return jnp.concatenate(
        [jnp.concatenate([re, -im], axis=1), jnp.concatenate([im, re], axis=1)], axis=0
    )


def apply(pair, operator):
    out = jnp.dot(pair, operator, preferred_element_type=jnp.float32)
    return out.astype(jnp.bfloat16)


def line_table(tie):
    k = jnp.arange(F, dtype=jnp.int32)[None, :] + tie
    a = jnp.arange(32, dtype=jnp.int32)[:, None]
    coarse = (a * 32 * k % F).astype(jnp.float32) * (2.0 * math.pi / F)
    fine = (a * k % F).astype(jnp.float32) * (2.0 * math.pi / F)
    ca, sa, cb, sb = lax.optimization_barrier(
        (jnp.cos(coarse), jnp.sin(coarse), jnp.cos(fine), jnp.sin(fine))
    )
    cos = ca[:, None, :] * cb[None, :, :] - sa[:, None, :] * sb[None, :, :]
    sin = sa[:, None, :] * cb[None, :, :] + ca[:, None, :] * sb[None, :, :]
    return jnp.stack([cos, sin]).astype(jnp.bfloat16).reshape(2 * F, F)


def line_weights(blocks, owned):
    u = 2.0 * np.pi * (np.outer(np.arange(blocks), np.arange(blocks)) % blocks) / blocks
    cos = np.cos(u).astype(np.float32)
    sin = np.sin(u).astype(np.float32)
    w = np.zeros((owned, 2, blocks, blocks, 2, owned), np.float32)
    for s in range(owned):
        w[s, 0, :, :, 0, s] = cos.T
        w[s, 0, :, :, 1, s] = sin.T
        w[s, 1, :, :, 1, s] = cos.T
        w[s, 1, :, :, 0, s] = -sin.T
    m = np.where(np.arange(blocks) < blocks // 2, np.arange(blocks), np.arange(blocks) - blocks)
    g = 0.5 * (1.0 + m / np.sqrt(m * m + 1.0))
    rows = np.broadcast_to(g[None, None, :], (owned, 2, blocks)).reshape(-1, 1)
    n = owned * 2 * blocks
    return jnp.asarray(w.reshape(n, n), jnp.bfloat16), jnp.asarray(rows, jnp.float32)


def shards(source, start_tick, op_x, op_y):
    nx, ny = lax.axis_size("bx"), lax.axis_size("by")
    i, j = lax.axis_index("bx"), lax.axis_index("by")
    src = source[0, 0].astype(jnp.float32)
    x_op = op_x.reshape(2 * F, F)
    y_op = op_y.reshape(2 * F, F)
    first = start_tick[0, 0]

    def inside(flag, value):
        return jnp.where(flag, value.astype(jnp.float32), 0.0)

    east = north = None
    table = None
    for tick in range(TICKS):
        own = jnp.where(first <= tick, src, 0.0)
        if tick == 0:
            incident = own.astype(jnp.bfloat16)
        else:
            incident = (inside(i > 0, from_west) + inside(j > 0, from_south) + own).astype(jnp.bfloat16)
        pair = lax.optimization_barrier(paired(incident))
        east = apply(pair, x_op).reshape(2, SHOTS, F)
        from_west = shift(east, "bx", 1)
        if tick == TICKS - 1:
            from_east = shift(east, "bx", -1)
        north = apply(pair, y_op).reshape(2, SHOTS, F)
        from_south = shift(north, "by", 1)
        if tick == TICKS - 1:
            from_north = shift(north, "by", -1)
        if tick == 1:
            tie = jnp.minimum(first, 0) * (pair[0, 0] > 1e30).astype(jnp.int32)
            table = line_table(tie)
    mismatch = (
        inside(i > 0, from_west)
        + inside(j > 0, from_south)
        - inside(i < nx - 1, from_east)
        - inside(j < ny - 1, from_north)
    ).astype(jnp.bfloat16)
    reflected = apply(lax.optimization_barrier(paired(mismatch)), x_op).reshape(2, SHOTS, F)
    re, im = reflected[0], reflected[1]
    turned = jnp.concatenate(
        [jnp.concatenate([re, im], axis=1), jnp.concatenate([im, -re], axis=1)], axis=0
    )
    spectrum = apply(lax.optimization_barrier(turned), table)
    owned = SHOTS // nx
    pieces = spectrum.reshape(2, nx, owned, F).transpose(1, 0, 2, 3).reshape(nx, 2 * owned, F)
    regrouped = lax.all_to_all(pieces, "bx", split_axis=0, concat_axis=0, tiled=True)
    weights, gain = line_weights(nx, owned)
    up = jnp.dot(weights, regrouped.reshape(nx * 2 * owned, F), preferred_element_type=jnp.float32)
    return (up * gain).reshape(1, owned, 2, nx, F)


def solution(mesh):
    placed = (
        P("bx", "by", None, None, None),
        P("bx", "by"),
        P("bx", "by", None, None, None),
        P("bx", "by", None, None, None),
    )
    return jax.shard_map(
        shards,
        mesh=mesh,
        in_specs=placed,
        out_specs=P("by", "bx", None, None, None),
        check_vma=False,
    )
```

time: 210 us -> 127 us (0.60)
  starting transfers between devices: 54.9 us -> 8.8 us
  matrix products: 47.9 us -> 14.9 us
  waiting for transfers between devices: 96.9 us -> 64.1 us
  blocking collectives: 0 us -> 21.7 us
  local copies, waits for them, and re-layouts: 1.61 us -> 7.54 us
    dot_general x24 -> x11, matrix products: 47.9 us -> 14.9 us  [the longest x10 13.6 us: apply(): out = jnp.dot(pair, operator, preferred_element_type=jnp.float32)]
    ppermute x10, starting transfers between devices: 34.9 us -> 8.8 us  [shift(): return lax.ppermute(value, axis, [(i, (i + by) % n) for i in range(n)])]
    all_to_all x0 -> x1, blocking collectives: none -> 21.7 us  [shards(): lax.all_to_all(pieces, 'bx', split_axis=0, concat_axis=0, tiled=True)]
    all_to_all x1 -> x0, starting transfers between devices: 20 us -> none  [shards(): lax.all_to_all(arranged, 'bx', split_axis=1, concat_axis=3, tiled=True)]
    all_to_all x1 -> x0, waiting for transfers between devices: 17.1 us -> none  [shards(): lax.all_to_all(arranged, 'bx', split_axis=1, concat_axis=3, tiled=True)]
    ppermute x10, waiting for transfers between devices: 79.8 us -> 64.1 us  [shift(): return lax.ppermute(value, axis, [(i, (i + by) % n) for i in range(n)])]
    unnamed x6 -> x18, local copies, waits for them, and re-layouts: 0.02 us -> 6.14 us
  transfers between devices with their start and end apart: 11 -> 10, of which waited for: 11 -> 9; matrix products, arithmetic and copies ran while one was open for 1% -> 4% of each run, Pallas kernels for 0% -> 0%
where the time goes in v1:
time: 127 us; the launch traced here: 125 us
  waiting for transfers between devices  64.1 us (50%)
  blocking collectives  21.7 us (17%)
  matrix products  14.9 us (12%)
  starting transfers between devices  8.8 us (7%)
  local copies, waits for them, and re-layouts  7.54 us (6%)
  other arithmetic  6.14 us (5%)
  between operations  1.67 us (1%)
    ppermute x10, waiting for transfers between devices, shift(): return lax.ppermute(value, axis, [(i, (i + by) % n) for i in range(n)])  64.1 us
    all_to_all x1, blocking collectives, shards(): lax.all_to_all(pieces, 'bx', split_axis=0, concat_axis=0, tiled=True)  21.7 us
    dot_general x10, matrix products, apply(): out = jnp.dot(pair, operator, preferred_element_type=jnp.float32)  13.6 us
    ppermute x10, starting transfers between devices, shift(): return lax.ppermute(value, axis, [(i, (i + by) % n) for i in range(n)])  8.8 us
    unnamed x18, local copies, waits for them, and re-layouts  6.14 us
  transfers between devices with their start and end apart: 10, of which 9 were waited for; matrix products, arithmetic and copies ran while one was open for 4% of the time, Pallas kernels for 0%

profile of v1, /device:TPU:3, one launch (start us, length us, event | category | flops | bytes accessed | tf_op | source)
XLA Modules:
  0.0 124.9 jit_solution(17474938159168016805)
XLA Ops:
  0.7 0.0 copy-start.3
  0.7 1.3 %fusion = bf16[1,1,2,128,1024]{4,3,2,1,0:T(8,128)(2,1)S(1)} fusion(bf16[1,1,2,128,1024]{4,3,2,1,0:T(8,128)(2,1)} %param.6, pred[]{:T(512)} %bitcast), kind=kLoop, calls=%fused_computation.18 | loop fusion | flops 786432 | bytes 1048577 | tf_op jit(solution)/shard_map/convert_element_type | solution.py:77
  2.0 0.1 maximum_maximum_fusion
  2.1 0.9 copy-done.3
  3.0 0.0 copy-start.6
  3.0 1.3 %convolution_convert_fusion.8 = bf16[256,1024]{1,0:T(8,128)(2,1)S(1)} fusion(bf16[256,2048]{1,0:T(8,128)(2,1)S(1)} %maximum_maximum_fusion, bf16[2048,1024]{1,0:T(8,128)(2,1)S(1)} %bitcast.96), kind=kOutput, calls=%fused_computation.16 | convolution fusion | flops 1074003968 | bytes 5767168 | tf_op jit(solution)/shard_map/dot_general | solution.py:27
  4.3 1.8 %collective-permute-start.1 = (bf16[2,128,1024]{2,1,0:T(8,128)(2,1)S(1)}, bf16[2,128,1024]{2,1,0:T(8,128)(2,1)S(1)}, u32[]{:S(2)}, u32[]{:S(2)}) collective-permute-start(bf16[2,128,1024]{2,1,0:T(8,128)(2,1)S(1)} %bitcast.110), channel_id=1, source_target_pairs={{0,1},{1,2},{2,3},{3,4},{4,5},{5,6},{6,7},{7,0},{8,9},{9,10},{10,1... | collective-permute-start | bytes 1572872 | tf_op jit(solution)/shard_map/ppermute | solution.py:16
  6.1 0.0 copy-done.6
  6.1 1.3 %convolution_convert_fusion.9 = bf16[256,1024]{1,0:T(8,128)(2,1)S(1)} fusion(bf16[256,2048]{1,0:T(8,128)(2,1)S(1)} %maximum_maximum_fusion, bf16[2048,1024]{1,0:T(8,128)(2,1)S(1)} %bitcast.100), kind=kOutput, calls=%fused_computation.17 | convolution fusion | flops 1074003968 | bytes 5767168 | tf_op jit(solution)/shard_map/dot_general | solution.py:27
  7.3 1.4 %collective-permute-start = (bf16[2,128,1024]{2,1,0:T(8,128)(2,1)S(1)}, bf16[2,128,1024]{2,1,0:T(8,128)(2,1)S(1)}, u32[]{:S(2)}, u32[]{:S(2)}) collective-permute-start(bf16[2,128,1024]{2,1,0:T(8,128)(2,1)S(1)} %bitcast.111), channel_id=1, source_target_pairs={{0,8},{8,16},{16,24},{24,32},{32,40},{40,48},{48,56},{56,64},{64,7... | collective-permute-start | bytes 1572872 | tf_op jit(solution)/shard_map/ppermute | solution.py:16
  8.7 3.5 %collective-permute-done.1 = bf16[2,128,1024]{2,1,0:T(8,128)(2,1)S(1)} collective-permute-done((bf16[2,128,1024]{2,1,0:T(8,128)(2,1)S(1)}, bf16[2,128,1024]{2,1,0:T(8,128)(2,1)S(1)}, u32[]{:S(2)}, u32[]{:S(2)}) %collective-permute-start.1) | collective-permute-done | bytes 524320 | tf_op jit(solution)/shard_map/ppermute | solution.py:16
  12.2 15.7 %collective-permute-done = bf16[2,128,1024]{2,1,0:T(8,128)(2,1)S(1)} collective-permute-done((bf16[2,128,1024]{2,1,0:T(8,128)(2,1)S(1)}, bf16[2,128,1024]{2,1,0:T(8,128)(2,1)S(1)}, u32[]{:S(2)}, u32[]{:S(2)}) %collective-permute-start) | collective-permute-done | bytes 524320 | tf_op jit(solution)/shard_map/ppermute | solution.py:16
  27.9 0.0 copy-done
  27.9 0.3 fusion.3
  28.3 0.1 maximum_maximum_fusion.1
  28.4 1.7 %copy-done.4 = bf16[1,1,2,1024,1024]{4,3,2,1,0:T(8,128)(2,1)S(1)} copy-done((bf16[1,1,2,1024,1024]{4,3,2,1,0:T(8,128)(2,1)S(1)}, bf16[1,1,2,1024,1024]{4,3,2,1,0:T(8,128)(2,1)}, u32[]{:S(2)}) %copy-start.4) | copy-done | bytes 4194328
  30.1 1.3 %convolution_convert_fusion.6 = bf16[256,1024]{1,0:T(8,128)(2,1)S(1)} fusion(bf16[256,2048]{1,0:T(8,128)(2,1)S(1)} %maximum_maximum_fusion.1, bf16[2048,1024]{1,0:T(8,128)(2,1)S(1)} %bitcast.97), kind=kOutput, calls=%fused_computation.14 | convolution fusion | flops 1074003968 | bytes 5767168 | tf_op jit(solution)/shard_map/dot_general | solution.py:27
  31.4 0.9 copy-done.7
  32.3 1.3 %convolution_convert_fusion.7 = bf16[256,1024]{1,0:T(8,128)(2,1)S(1)} fusion(bf16[256,2048]{1,0:T(8,128)(2,1)S(1)} %maximum_maximum_fusion.1, bf16[2048,1024]{1,0:T(8,128)(2,1)S(1)} %bitcast.101), kind=kOutput, calls=%fused_computation.15 | convolution fusion | flops 1074003968 | bytes 5767168 | tf_op jit(solution)/shard_map/dot_general | solution.py:27
  33.6 1.2 collective-permute-start.3
  34.8 0.0 collective-permute-start.2
  34.8 6.1 %collective-permute-done.3 = bf16[2,128,1024]{2,1,0:T(8,128)(2,1)S(1)} collective-permute-done((bf16[2,128,1024]{2,1,0:T(8,128)(2,1)S(1)}, bf16[2,128,1024]{2,1,0:T(8,128)(2,1)S(1)}, u32[]{:S(2)}, u32[]{:S(2)}) %collective-permute-start.3) | collective-permute-done | bytes 524320 | tf_op jit(solution)/shard_map/ppermute | solution.py:16
  40.9 10.6 %collective-permute-done.2 = bf16[2,128,1024]{2,1,0:T(8,128)(2,1)S(1)} collective-permute-done((bf16[2,128,1024]{2,1,0:T(8,128)(2,1)S(1)}, bf16[2,128,1024]{2,1,0:T(8,128)(2,1)S(1)}, u32[]{:S(2)}, u32[]{:S(2)}) %collective-permute-start.2) | collective-permute-done | bytes 524320 | tf_op jit(solution)/shard_map/ppermute | solution.py:16
  51.5 0.3 fusion.6
  51.9 0.1 maximum_maximum_fusion.2
  52.0 2.1 %convolution_convert_fusion.4 = bf16[256,1024]{1,0:T(8,128)(2,1)} fusion(bf16[256,2048]{1,0:T(8,128)(2,1)S(1)} %maximum_maximum_fusion.2, bf16[2048,1024]{1,0:T(8,128)(2,1)S(1)} %bitcast.98), kind=kOutput, calls=%fused_computation.12 | convolution fusion | flops 1074003968 | bytes 5767168 | tf_op jit(solution)/shard_map/dot_general | solution.py:27
  54.1 1.3 %convolution_convert_fusion.5 = bf16[256,1024]{1,0:T(8,128)(2,1)S(1)} fusion(bf16[256,2048]{1,0:T(8,128)(2,1)S(1)} %maximum_maximum_fusion.2, bf16[2048,1024]{1,0:T(8,128)(2,1)S(1)} %bitcast.102), kind=kOutput, calls=%fused_computation.13 | convolution fusion | flops 1074003968 | bytes 5767168 | tf_op jit(solution)/shard_map/dot_general | solution.py:27
  55.4 1.2 collective-permute-start.5
  56.5 0.0 collective-permute-start.4
  56.5 0.6 slice.68
  57.8 1.1 fusion.22
  58.9 4.1 %collective-permute-done.5 = bf16[2,128,1024]{2,1,0:T(8,128)(2,1)S(1)} collective-permute-done((bf16[2,128,1024]{2,1,0:T(8,128)(2,1)}, bf16[2,128,1024]{2,1,0:T(8,128)(2,1)S(1)}, u32[]{:S(2)}, u32[]{:S(2)}) %collective-permute-start.5) | collective-permute-done | bytes 524320 | tf_op jit(solution)/shard_map/ppermute | solution.py:16
  63.0 10.8 %collective-permute-done.4 = bf16[2,128,1024]{2,1,0:T(8,128)(2,1)S(1)} collective-permute-done((bf16[2,128,1024]{2,1,0:T(8,128)(2,1)S(1)}, bf16[2,128,1024]{2,1,0:T(8,128)(2,1)S(1)}, u32[]{:S(2)}, u32[]{:S(2)}) %collective-permute-start.4) | collective-permute-done | bytes 524320 | tf_op jit(solution)/shard_map/ppermute | solution.py:16
  73.7 0.3 fusion.9
  74.1 0.1 maximum_maximum_fusion.3
  74.2 1.7 %copy-done.5 = bf16[1,1,2,1024,1024]{4,3,2,1,0:T(8,128)(2,1)S(1)} copy-done((bf16[1,1,2,1024,1024]{4,3,2,1,0:T(8,128)(2,1)S(1)}, bf16[1,1,2,1024,1024]{4,3,2,1,0:T(8,128)(2,1)}, u32[]{:S(2)}) %copy-start.5) | copy-done | bytes 4194328
  75.9 1.3 %convolution_convert_fusion.2 = bf16[256,1024]{1,0:T(8,128)(2,1)S(1)} fusion(bf16[256,2048]{1,0:T(8,128)(2,1)S(1)} %maximum_maximum_fusion.3, bf16[2048,1024]{1,0:T(8,128)(2,1)S(1)} %bitcast.99), kind=kOutput, calls=%fused_computation.10 | convolution fusion | flops 1074003968 | bytes 5767168 | tf_op jit(solution)/shard_map/dot_general | solution.py:27
  77.2 0.9 copy-done.8
  78.1 1.3 %convolution_convert_fusion.3 = bf16[256,1024]{1,0:T(8,128)(2,1)S(1)} fusion(bf16[256,2048]{1,0:T(8,128)(2,1)S(1)} %maximum_maximum_fusion.3, bf16[2048,1024]{1,0:T(8,128)(2,1)S(1)} %bitcast.103), kind=kOutput, calls=%fused_computation.11 | convolution fusion | flops 1074003968 | bytes 5767168 | tf_op jit(solution)/shard_map/dot_general | solution.py:27
  79.4 0.4 collective-permute-start.9
  79.8 1.4 %collective-permute-start.7 = (bf16[2,128,1024]{2,1,0:T(8,128)(2,1)S(1)}, bf16[2,128,1024]{2,1,0:T(8,128)(2,1)S(1)}, u32[]{:S(2)}, u32[]{:S(2)}) collective-permute-start(bf16[2,128,1024]{2,1,0:T(8,128)(2,1)S(1)} %bitcast.109), channel_id=1, source_target_pairs={{0,1},{1,2},{2,3},{3,4},{4,5},{5,6},{6,7},{7,0},{8,9},{9,10},{10,1... | collective-permute-start | bytes 1572872 | tf_op jit(solution)/shard_map/ppermute | solution.py:16
  81.2 0.0 collective-permute-start.8
  81.2 1.5 %collective-permute-start.6 = (bf16[2,128,1024]{2,1,0:T(8,128)(2,1)S(1)}, bf16[2,128,1024]{2,1,0:T(8,128)(2,1)S(1)}, u32[]{:S(2)}, u32[]{:S(2)}) collective-permute-start(bf16[2,128,1024]{2,1,0:T(8,128)(2,1)S(1)} %bitcast.107), channel_id=1, source_target_pairs={{0,8},{8,16},{16,24},{24,32},{32,40},{40,48},{48,56},{56,64},{64,7... | collective-permute-start | bytes 1572872 | tf_op jit(solution)/shard_map/ppermute | solution.py:16
  82.6 1.4 %subtract_convert_fusion = (bf16[1,32,32,1024]{3,2,1,0:T(8,128)(2,1)S(1)}, bf16[1,32,32,1024]{3,2,1,0:T(8,128)(2,1)S(1)}) fusion(f32[32,1024]{1,0:T(8,128)S(1)} %get-tuple-element.12, f32[32,1024]{1,0:T(8,128)S(1)} %get-tuple-element.11, f32[32,1024]{1,0:T(8,128)S(1)} %get-tuple-element.10, f32[32,1024]{1,0:T(8,128)S(1)} %get-tuple-element.9), kind=kLoop, calls=%fused_computation.2 | loop fusion | flops 8388608 | bytes 4718592 | tf_op jit(solution)/shard_map/convert
  84.0 0.4 pad_maximum_fusion
  84.4 3.9 %collective-permute-done.9 = bf16[2,128,1024]{2,1,0:T(8,128)(2,1)S(1)} collective-permute-done((bf16[2,128,1024]{2,1,0:T(8,128)(2,1)S(1)}, bf16[2,128,1024]{2,1,0:T(8,128)(2,1)S(1)}, u32[]{:S(2)}, u32[]{:S(2)}) %collective-permute-start.9) | collective-permute-done | bytes 524320 | tf_op jit(solution)/shard_map/ppermute | solution.py:16
  88.3 0.0 collective-permute-done.7
  88.3 6.4 %collective-permute-done.8 = bf16[2,128,1024]{2,1,0:T(8,128)(2,1)S(1)} collective-permute-done((bf16[2,128,1024]{2,1,0:T(8,128)(2,1)S(1)}, bf16[2,128,1024]{2,1,0:T(8,128)(2,1)S(1)}, u32[]{:S(2)}, u32[]{:S(2)}) %collective-permute-start.8) | collective-permute-done | bytes 524320 | tf_op jit(solution)/shard_map/ppermute | solution.py:16
  94.7 3.0 %collective-permute-done.6 = bf16[2,128,1024]{2,1,0:T(8,128)(2,1)S(1)} collective-permute-done((bf16[2,128,1024]{2,1,0:T(8,128)(2,1)S(1)}, bf16[2,128,1024]{2,1,0:T(8,128)(2,1)S(1)}, u32[]{:S(2)}, u32[]{:S(2)}) %collective-permute-start.6) | collective-permute-done | bytes 524320 | tf_op jit(solution)/shard_map/ppermute | solution.py:16
  97.7 0.4 subtract_convert_fusion.1
  98.3 0.1 maximum_maximum_fusion.4
  98.3 1.3 %convolution_convert_fusion.1 = bf16[256,1024]{1,0:T(8,128)(2,1)S(1)} fusion(bf16[256,2048]{1,0:T(8,128)(2,1)S(1)} %maximum_maximum_fusion.4, bf16[2048,1024]{1,0:T(8,128)(2,1)S(1)} %bitcast.104), kind=kOutput, calls=%fused_computation.9 | convolution fusion | flops 1074003968 | bytes 5767168 | tf_op jit(solution)/shard_map/dot_general | solution.py:27
  99.7 0.1 fusion.29
  99.7 0.1 maximum_maximum_fusion.5
  99.8 1.3 %convolution_convert_fusion = bf16[256,1024]{1,0:T(8,128)(2,1)S(1)} fusion(bf16[256,2048]{1,0:T(8,128)(2,1)S(1)} %maximum_maximum_fusion.5, bf16[2048,1024]{1,0:T(8,128)(2,1)S(1)} %bitcast.94), kind=kOutput, calls=%fused_computation.8 | convolution fusion | flops 1074003968 | bytes 5767168 | tf_op jit(solution)/shard_map/dot_general | solution.py:27
  101.1 0.0 copy-start.1
  101.2 0.0 copy-start.2
  101.2 0.2 reshape.124
  101.4 0.2 copy.10
  101.5 0.3 copy.11
  101.8 21.7 %all_to_all.5 = bf16[32,8,1024]{2,1,0:T(8,128)(2,1)S(1)} all-to-all(bf16[32,8,1024]{2,1,0:T(8,128)(2,1)S(1)} %copy.11), channel_id=1, replica_groups=mesh['bx'=32,'by'=8] {'bx'}, dimensions={0} | all-to-all | bytes 1048576 | tf_op jit(solution)/shard_map/all_to_all | solution.py:106
  123.6 0.0 copy-done.1
  123.6 0.0 copy-done.2
  123.6 1.3 %convolution_multiply_fusion = f32[1024,256]{0,1:T(8,128)} fusion(bf16[256,256]{1,0:T(8,128)(2,1)S(1)} %copy-done.1, bf16[32,8,1024]{2,1,0:T(8,128)(2,1)S(1)} %all_to_all.5, f32[256]{0:T(256)S(1)} %copy-done.2), kind=kOutput, calls=%fused_computation.7 | convolution fusion | flops 134479872 | bytes 1704960 | tf_op jit(solution)/shard_map/dot_general | solution.py:108
  (17 shorter events, 0.3 us)
Async XLA Ops:
  0.7 2.3 %copy-start.3 = (bf16[1,1,2,1024,1024]{4,3,2,1,0:T(8,128)(2,1)S(1)}, bf16[1,1,2,1024,1024]{4,3,2,1,0:T(8,128)(2,1)}, u32[]{:S(2)}) copy-start(bf16[1,1,2,1024,1024]{4,3,2,1,0:T(8,128)(2,1)} %param.9) | copy-start | bytes 12582916
  3.0 3.1 %copy-start.6 = (bf16[1,1,2,1024,1024]{4,3,2,1,0:T(8,128)(2,1)S(1)}, bf16[1,1,2,1024,1024]{4,3,2,1,0:T(8,128)(2,1)}, u32[]{:S(2)}) copy-start(bf16[1,1,2,1024,1024]{4,3,2,1,0:T(8,128)(2,1)} %param.8) | copy-start | bytes 12582916
  4.3 7.9 %collective-permute-start.1 = (bf16[2,128,1024]{2,1,0:T(8,128)(2,1)S(1)}, bf16[2,128,1024]{2,1,0:T(8,128)(2,1)S(1)}, u32[]{:S(2)}, u32[]{:S(2)}) collective-permute-start(bf16[2,128,1024]{2,1,0:T(8,128)(2,1)S(1)} %bitcast.110), channel_id=1, source_target_pairs={{0,1},{1,2},{2,3},{3,4},{4,5},{5,6},{6,7},{7,0},{8,9},{9,10},{10,1... | collective-permute-start | bytes 1572872 | tf_op jit(solution)/shard_map/ppermute | solution.py:16
  6.1 21.8 %copy-start = (bf16[1,1,2,128,1024]{4,3,2,1,0:T(8,128)(2,1)S(1)}, bf16[1,1,2,128,1024]{4,3,2,1,0:T(8,128)(2,1)}, u32[]{:S(2)}) copy-start(bf16[1,1,2,128,1024]{4,3,2,1,0:T(8,128)(2,1)} %param.6) | copy-start | bytes 1572868
  7.3 20.5 %collective-permute-start = (bf16[2,128,1024]{2,1,0:T(8,128)(2,1)S(1)}, bf16[2,128,1024]{2,1,0:T(8,128)(2,1)S(1)}, u32[]{:S(2)}, u32[]{:S(2)}) collective-permute-start(bf16[2,128,1024]{2,1,0:T(8,128)(2,1)S(1)} %bitcast.111), channel_id=1, source_target_pairs={{0,8},{8,16},{16,24},{24,32},{32,40},{40,48},{48,56},{56,64},{64,7... | collective-permute-start | bytes 1572872 | tf_op jit(solution)/shard_map/ppermute | solution.py:16
  27.9 2.2 %copy-start.4 = (bf16[1,1,2,1024,1024]{4,3,2,1,0:T(8,128)(2,1)S(1)}, bf16[1,1,2,1024,1024]{4,3,2,1,0:T(8,128)(2,1)}, u32[]{:S(2)}) copy-start(bf16[1,1,2,1024,1024]{4,3,2,1,0:T(8,128)(2,1)} %param.9) | copy-start | bytes 12582916
  30.1 2.2 %copy-start.7 = (bf16[1,1,2,1024,1024]{4,3,2,1,0:T(8,128)(2,1)S(1)}, bf16[1,1,2,1024,1024]{4,3,2,1,0:T(8,128)(2,1)}, u32[]{:S(2)}) copy-start(bf16[1,1,2,1024,1024]{4,3,2,1,0:T(8,128)(2,1)} %param.8) | copy-start | bytes 12582916
  33.6 7.4 %collective-permute-start.3 = (bf16[2,128,1024]{2,1,0:T(8,128)(2,1)S(1)}, bf16[2,128,1024]{2,1,0:T(8,128)(2,1)S(1)}, u32[]{:S(2)}, u32[]{:S(2)}) collective-permute-start(bf16[2,128,1024]{2,1,0:T(8,128)(2,1)S(1)} %bitcast.113), channel_id=1, source_target_pairs={{0,1},{1,2},{2,3},{3,4},{4,5},{5,6},{6,7},{7,0},{8,9},{9,10},{10,1... | collective-permute-start | bytes 1572872 | tf_op jit(solution)/shard_map/ppermute | solution.py:16
  34.8 16.7 %collective-permute-start.2 = (bf16[2,128,1024]{2,1,0:T(8,128)(2,1)S(1)}, bf16[2,128,1024]{2,1,0:T(8,128)(2,1)S(1)}, u32[]{:S(2)}, u32[]{:S(2)}) collective-permute-start(bf16[2,128,1024]{2,1,0:T(8,128)(2,1)S(1)} %bitcast.112), channel_id=1, source_target_pairs={{0,8},{8,16},{16,24},{24,32},{32,40},{40,48},{48,56},{56,64},{64,7... | collective-permute-start | bytes 1572872 | tf_op jit(solution)/shard_map/ppermute | solution.py:16
  55.4 7.6 %collective-permute-start.5 = (bf16[2,128,1024]{2,1,0:T(8,128)(2,1)}, bf16[2,128,1024]{2,1,0:T(8,128)(2,1)S(1)}, u32[]{:S(2)}, u32[]{:S(2)}) collective-permute-start(bf16[2,128,1024]{2,1,0:T(8,128)(2,1)} %bitcast.18), channel_id=1, source_target_pairs={{0,1},{1,2},{2,3},{3,4},{4,5},{5,6},{6,7},{7,0},{8,9},{9,10},{10,1... | collective-permute-start | bytes 1572872 | tf_op jit(solution)/shard_map/ppermute | solution.py:16
  56.5 17.2 %collective-permute-start.4 = (bf16[2,128,1024]{2,1,0:T(8,128)(2,1)S(1)}, bf16[2,128,1024]{2,1,0:T(8,128)(2,1)S(1)}, u32[]{:S(2)}, u32[]{:S(2)}) collective-permute-start(bf16[2,128,1024]{2,1,0:T(8,128)(2,1)S(1)} %bitcast.105), channel_id=1, source_target_pairs={{0,8},{8,16},{16,24},{24,32},{32,40},{40,48},{48,56},{56,64},{64,7... | collective-permute-start | bytes 1572872 | tf_op jit(solution)/shard_map/ppermute | solution.py:16
  73.7 2.2 %copy-start.5 = (bf16[1,1,2,1024,1024]{4,3,2,1,0:T(8,128)(2,1)S(1)}, bf16[1,1,2,1024,1024]{4,3,2,1,0:T(8,128)(2,1)}, u32[]{:S(2)}) copy-start(bf16[1,1,2,1024,1024]{4,3,2,1,0:T(8,128)(2,1)} %param.9) | copy-start | bytes 12582916
  75.9 2.2 %copy-start.8 = (bf16[1,1,2,1024,1024]{4,3,2,1,0:T(8,128)(2,1)S(1)}, bf16[1,1,2,1024,1024]{4,3,2,1,0:T(8,128)(2,1)}, u32[]{:S(2)}) copy-start(bf16[1,1,2,1024,1024]{4,3,2,1,0:T(8,128)(2,1)} %param.8) | copy-start | bytes 12582916
  79.4 8.9 %collective-permute-start.9 = (bf16[2,128,1024]{2,1,0:T(8,128)(2,1)S(1)}, bf16[2,128,1024]{2,1,0:T(8,128)(2,1)S(1)}, u32[]{:S(2)}, u32[]{:S(2)}) collective-permute-start(bf16[2,128,1024]{2,1,0:T(8,128)(2,1)S(1)} %bitcast.108), channel_id=1, source_target_pairs={{0,7},{1,0},{2,1},{3,2},{4,3},{5,4},{6,5},{7,6},{8,15},{9,8},{10,9... | collective-permute-start | bytes 1572872 | tf_op jit(solution)/shard_map/ppermute | solution.py:16
  79.8 8.5 %collective-permute-start.7 = (bf16[2,128,1024]{2,1,0:T(8,128)(2,1)S(1)}, bf16[2,128,1024]{2,1,0:T(8,128)(2,1)S(1)}, u32[]{:S(2)}, u32[]{:S(2)}) collective-permute-start(bf16[2,128,1024]{2,1,0:T(8,128)(2,1)S(1)} %bitcast.109), channel_id=1, source_target_pairs={{0,1},{1,2},{2,3},{3,4},{4,5},{5,6},{6,7},{7,0},{8,9},{9,10},{10,1... | collective-permute-start | bytes 1572872 | tf_op jit(solution)/shard_map/ppermute | solution.py:16
  81.2 13.6 %collective-permute-start.8 = (bf16[2,128,1024]{2,1,0:T(8,128)(2,1)S(1)}, bf16[2,128,1024]{2,1,0:T(8,128)(2,1)S(1)}, u32[]{:S(2)}, u32[]{:S(2)}) collective-permute-start(bf16[2,128,1024]{2,1,0:T(8,128)(2,1)S(1)} %bitcast.106), channel_id=1, source_target_pairs={{0,248},{8,0},{16,8},{24,16},{32,24},{40,32},{48,40},{56,48},{64,5... | collective-permute-start | bytes 1572872 | tf_op jit(solution)/shard_map/ppermute | solution.py:16
  81.2 16.6 %collective-permute-start.6 = (bf16[2,128,1024]{2,1,0:T(8,128)(2,1)S(1)}, bf16[2,128,1024]{2,1,0:T(8,128)(2,1)S(1)}, u32[]{:S(2)}, u32[]{:S(2)}) collective-permute-start(bf16[2,128,1024]{2,1,0:T(8,128)(2,1)S(1)} %bitcast.107), channel_id=1, source_target_pairs={{0,8},{8,16},{16,24},{24,32},{32,40},{40,48},{48,56},{56,64},{64,7... | collective-permute-start | bytes 1572872 | tf_op jit(solution)/shard_map/ppermute | solution.py:16
  101.1 22.4 %copy-start.1 = (bf16[256,256]{1,0:T(8,128)(2,1)S(1)}, bf16[256,256]{1,0:T(8,128)(2,1)}, u32[]{:S(2)}) copy-start(bf16[256,256]{1,0:T(8,128)(2,1)} %constant.61.clone) | copy-start | bytes 393220
  101.2 22.4 %copy-start.2 = (f32[256]{0:T(256)S(1)}, f32[256]{0:T(256)}, u32[]{:S(2)}) copy-start(f32[256]{0:T(256)} %constant.67) | copy-start | bytes 3076

commit v2 on v1

v2 whole, which is shorter than its diff:
```python
import functools

import jax
import jax.numpy as jnp
import numpy as np
from jax import lax
from jax.experimental import pallas as pl
from jax.experimental.pallas import tpu as pltpu
from jax.sharding import PartitionSpec as P


F = 1024
TICKS = 4
SHOTS = 128
CUTS = (0, 64, 128)
CHUNKS = len(CUTS) - 1
STEP = 512
BF16 = jnp.bfloat16
F32 = jnp.float32
MIB = 1 << 20


def shift(value, axis, by):
    n = lax.axis_size(axis)
    return lax.ppermute(value, axis, [(i, (i + by) % n) for i in range(n)])


def vmem():
    return pl.BlockSpec(memory_space=pltpu.VMEM)


def smem():
    return pl.BlockSpec(memory_space=pltpu.SMEM)


def anywhere():
    return pl.BlockSpec(memory_space=pl.ANY)


def call(kernel, outs, specs, args, flops, scratch=(), limit=12):
    return pl.pallas_call(
        kernel,
        out_shape=[jax.ShapeDtypeStruct(shape, kind) for shape, kind in outs],
        in_specs=specs,
        out_specs=[vmem() for _ in outs],
        scratch_shapes=list(scratch),
        compiler_params=pltpu.CompilerParams(vmem_limit_bytes=limit * MIB),
        cost_estimate=pl.CostEstimate(flops=flops, bytes_accessed=MIB, transcendentals=0),
    )(*args)


def product(pair, operator, out):
    w = out.shape[1]
    for c in range(0, F, STEP):
        total = jnp.dot(pair[:, :F], operator[0, :, c : c + STEP], preferred_element_type=F32)
        total += jnp.dot(pair[:, F:], operator[1, :, c : c + STEP], preferred_element_type=F32)
        out[0, :, c : c + STEP] = total[:w].astype(BF16)
        out[1, :, c : c + STEP] = total[w:].astype(BF16)


def fill(pair, re, im):
    w = re.shape[0]
    pair[:w, :F] = re.astype(BF16)
    pair[:w, F:] = (-im).astype(BF16)
    pair[w:, :F] = im.astype(BF16)
    pair[w:, F:] = re.astype(BF16)


def wide(flag, value):
    return jnp.where(flag != 0, value.astype(F32), 0.0)


def east_kernel(tick, lo, hi, flags, *refs):
    if tick == 0:
        src, op, _, out, pair = refs
        parts = [wide(flags[0] <= tick, src[c, lo:hi]) for c in range(2)]
    else:
        src, west, south, op, _, out, pair = refs
        parts = [
            wide(flags[1], west[c]) + wide(flags[2], south[c]) + wide(flags[0] <= tick, src[c, lo:hi])
            for c in range(2)
        ]
    fill(pair, *parts)
    product(pair, op, out)


def north_kernel(pair, op, out):
    product(pair, op, out)


def table_kernel(coarse, fine, _, out):
    for a in range(32):
        ca, sa = coarse[0, a : a + 1, :], coarse[1, a : a + 1, :]
        cb, sb = fine[0], fine[1]
        out[0, 32 * a : 32 * a + 32, :] = (ca * cb - sa * sb).astype(BF16)
        out[1, 32 * a : 32 * a + 32, :] = (sa * cb + ca * sb).astype(BF16)


def mirror_kernel(flags, west, south, east, north, op, table, _, out, pair, refl):
    parts = [
        wide(flags[1], west[c])
        + wide(flags[2], south[c])
        - wide(flags[3], east[c])
        - wide(flags[4], north[c])
        for c in range(2)
    ]
    fill(pair, *parts)
    product(pair, op, refl)
    w = refl.shape[1]
    re, im = refl[0], refl[1]
    pair[:w, :F] = re
    pair[:w, F:] = im
    pair[w:, :F] = im
    pair[w:, F:] = -re
    product(pair, table, refl)
    r = lax.broadcasted_iota(jnp.int32, (2 * w, 2 * w), 0)
    k = lax.broadcasted_iota(jnp.int32, (2 * w, 2 * w), 1)
    from_row = (r % 8) // 4 * w + r // 8 * 4 + r % 4
    pick = jnp.where(k == from_row, 1.0, 0.0).astype(BF16)
    for c in range(0, F, STEP):
        rows = jnp.concatenate([refl[0, :, c : c + STEP], refl[1, :, c : c + STEP]], axis=0)
        moved = jnp.dot(pick, rows, preferred_element_type=F32).astype(BF16)
        out[:, :, c : c + STEP] = moved.reshape(w // 4, 8, STEP)


def last_kernel(weights, gain, got, out):
    out[...] = jnp.dot(weights[...], got[...], preferred_element_type=F32) * gain[...]


def line_parts():
    k = np.arange(F, dtype=np.int64)[None, :]
    a = np.arange(32, dtype=np.int64)[:, None]
    coarse = 2.0 * np.pi / F * (a * 32 * k % F)
    fine = 2.0 * np.pi / F * (a * k % F)
    pack = lambda t: jnp.asarray(np.stack([np.cos(t), np.sin(t)]).astype(np.float32))
    return pack(coarse), pack(fine)


def line_weights(blocks, owned):
    u = 2.0 * np.pi * (np.outer(np.arange(blocks), np.arange(blocks)) % blocks) / blocks
    cos = np.cos(u).astype(np.float32)
    sin = np.sin(u).astype(np.float32)
    w = np.zeros((owned, 2, blocks, blocks, 2, owned), np.float32)
    for s in range(owned):
        w[s, 0, :, :, 0, s] = cos.T
        w[s, 0, :, :, 1, s] = sin.T
        w[s, 1, :, :, 1, s] = cos.T
        w[s, 1, :, :, 0, s] = -sin.T
    m = np.where(np.arange(blocks) < blocks // 2, np.arange(blocks), np.arange(blocks) - blocks)
    g = 0.5 * (1.0 + m / np.sqrt(m * m + 1.0))
    n = owned * 2 * blocks
    gain = np.broadcast_to(g[None, None, :, None], (owned, 2, blocks, F)).reshape(n, F)[:, :1]
    return jnp.asarray(w.reshape(n, n), BF16), jnp.asarray(gain, F32)


def shards(source, start_tick, op_x, op_y):
    nx, ny = lax.axis_size("bx"), lax.axis_size("by")
    i, j = lax.axis_index("bx"), lax.axis_index("by")
    src, x_op, y_op = source[0, 0], op_x[0, 0], op_y[0, 0]
    flags = jnp.stack(
        [
            start_tick[0, 0],
            (i > 0).astype(jnp.int32),
            (j > 0).astype(jnp.int32),
            (i < nx - 1).astype(jnp.int32),
            (j < ny - 1).astype(jnp.int32),
        ]
    )
    coarse, fine = line_parts()
    west, south, ahead, above = ([None] * CHUNKS for _ in range(4))
    last = start_tick
    table = None
    sizes = []
    for lo, hi in zip(CUTS[:-1], CUTS[1:]):
        w = hi - lo
        sizes.append((w, ((2, w, F), BF16), ((2 * w, 2 * F), BF16), 2 * (2 * w) * (2 * F) * F))
    for tick in range(TICKS):
        for c in range(CHUNKS):
            w, trace, paired, flops = sizes[c]
            body = functools.partial(east_kernel, tick, CUTS[c], CUTS[c + 1])
            if tick == 0:
                specs = [smem(), vmem(), vmem(), anywhere()]
                args = [flags, src, x_op, last]
            else:
                specs = [smem(), vmem(), vmem(), vmem(), vmem(), anywhere()]
                args = [flags, src, west[c], south[c], x_op, last]
            east, pair = call(body, [trace, paired], specs, args, flops)
            west[c] = shift(east, "bx", 1)
            if tick == TICKS - 1:
                ahead[c] = shift(east, "bx", -1)
            (north,) = call(north_kernel, [trace], [vmem(), vmem()], [pair, y_op], flops)
            south[c] = shift(north, "by", 1)
            if tick == TICKS - 1:
                above[c] = shift(north, "by", -1)
            last = north
        if tick == 1:
            (table,) = call(
                table_kernel, [((2, F, F), BF16)], [vmem(), vmem(), anywhere()], [coarse, fine, last], flops
            )
            last = table
    owned = SHOTS // nx
    spectra = []
    for c in range(CHUNKS):
        w, trace, paired, flops = sizes[c]
        (piece,) = call(
            mirror_kernel,
            [((w // owned, 2 * owned, F), BF16)],
            [smem()] + [vmem()] * 6 + [anywhere()],
            [flags, west[c], south[c], ahead[c], above[c], x_op, table, last],
            2 * flops,
            [pltpu.VMEM(paired[0], BF16), pltpu.VMEM(trace[0], BF16)],
        )
        spectra.append(piece)
        last = piece
    pieces = jnp.concatenate(spectra, axis=0)
    regrouped = lax.all_to_all(pieces, "bx", split_axis=0, concat_axis=0, tiled=True)
    weights, gain = line_weights(nx, owned)
    (up,) = call(
        last_kernel,
        [((nx * 2 * owned, F), F32)],
        [vmem()] * 3,
        [weights, gain, regrouped.reshape(nx * 2 * owned, F)],
        1 << 27,
    )
    return up.reshape(1, owned, 2, nx, F)


def solution(mesh):
    placed = (
        P("bx", "by", None, None, None),
        P("bx", "by"),
        P("bx", "by", None, None, None),
        P("bx", "by", None, None, None),
    )

    return jax.shard_map(
        shards,
        mesh=mesh,
        in_specs=placed,
        out_specs=P("by", "bx", None, None, None),
        check_vma=False,
    )
```

time: 127 us -> 107 us (0.84)
  the two profiles are of different devices: /device:TPU:3 before, /device:TPU:6 now
where the time goes in v2:
time: 107 us; the launch traced here: 106 us
  waiting for transfers between devices  34.9 us (33%)
  blocking collectives  27 us (25%)
  Pallas kernels  22.8 us (21%)
  starting transfers between devices  15 us (14%)
  local copies, waits for them, and re-layouts  5.67 us (5%)
    ppermute x20, waiting for transfers between devices, shift(): return lax.ppermute(value, axis, [(i, (i + by) % n) for i in range(n)])  34.9 us
    all_to_all x1, blocking collectives, shards(): lax.all_to_all(pieces, 'bx', split_axis=0, concat_axis=0, tiled=True)  27 us
    pallas_call x20, Pallas kernels, call(): pl.pallas_call(kernel, out_shape=[jax.ShapeDtypeStruct(shape, kind) for s...  22.8 us
    ppermute x20, starting transfers between devices, shift(): return lax.ppermute(value, axis, [(i, (i + by) % n) for i in range(n)])  15 us
    unnamed x20, local copies, waits for them, and re-layouts  5.59 us
  transfers between devices with their start and end apart: 20, of which 10 were waited for; matrix products, arithmetic and copies ran while one was open for 0% of the time, Pallas kernels for 16%

profile of v2, /device:TPU:6, one launch (start us, length us, event | category | flops | bytes accessed | tf_op | source)
XLA Modules:
  0.0 106.4 jit_solution(2259000400961748309)
XLA Ops:
  0.7 0.1 stack.35.flags
  0.7 2.2 %copy-done = bf16[1,1,2,1024,1024]{4,3,2,1,0:T(8,128)(2,1)S(1)} copy-done((bf16[1,1,2,1024,1024]{4,3,2,1,0:T(8,128)(2,1)S(1)}, bf16[1,1,2,1024,1024]{4,3,2,1,0:T(8,128)(2,1)}, u32[]{:S(2)}) %copy-start) | copy-done | bytes 4194328
  2.9 1.0 copy-done.4
  4.0 1.3 %shard_map.82 = (bf16[2,64,1024]{2,1,0:T(8,128)(2,1)S(1)}, bf16[128,2048]{1,0:T(8,128)(2,1)S(1)}) custom-call(s32[5]{0:T(128)S(1)} %stack.35.flags, bf16[2,128,1024]{2,1,0:T(8,128)(2,1)S(1)} %bitcast.29, bf16[2,1024,1024]{2,1,0:T(8,128)(2,1)S(1)} %bitcast.11, s32[1,1]{1,0:T(1,128)} %copy.9.refs_2_), custom_call_target="tpu_custom_call" | custom-call | flops 536870912 | bytes 1048576 | tf_op jit(solution)/shard_map/pallas_call | solution.py:41
  5.2 0.0 copy-start.2
  5.3 2.3 %copy-done.2 = bf16[1,1,2,1024,1024]{4,3,2,1,0:T(8,128)(2,1)S(1)} copy-done((bf16[1,1,2,1024,1024]{4,3,2,1,0:T(8,128)(2,1)S(1)}, bf16[1,1,2,1024,1024]{4,3,2,1,0:T(8,128)(2,1)}, u32[]{:S(2)}) %copy-start.2) | copy-done | bytes 4194328
  7.6 0.7 shard_map.83.refs_2_
  8.3 0.0 collective-permute-start.1
  8.3 1.6 %collective-permute-start = (bf16[2,64,1024]{2,1,0:T(8,128)(2,1)S(1)}, bf16[2,64,1024]{2,1,0:T(8,128)(2,1)S(1)}, u32[]{:S(2)}, u32[]{:S(2)}) collective-permute-start(bf16[2,64,1024]{2,1,0:T(8,128)(2,1)S(1)} %get-tuple-element.21), channel_id=1, source_target_pairs={{0,8},{8,16},{16,24},{24,32},{32,40},{40,48},{48,56},{56,64},{64,7... | collective-permute-start | bytes 786440 | tf_op jit(solution)/shard_map/ppermute | solution.py:25
  10.0 1.3 %shard_map.84 = (bf16[2,64,1024]{2,1,0:T(8,128)(2,1)S(1)}, bf16[128,2048]{1,0:T(8,128)(2,1)S(1)}) custom-call(s32[5]{0:T(128)S(1)} %stack.35.flags, bf16[2,128,1024]{2,1,0:T(8,128)(2,1)S(1)} %bitcast.30, bf16[2,1024,1024]{2,1,0:T(8,128)(2,1)S(1)} %bitcast.12, bf16[2,64,1024]{2,1,0:T(8,128)(2,1)S(1)} %shard_map.83.refs_2_), custom_call_target="tpu_custom_call" | custom-call | flops 536870912 | bytes 1048576 | tf_op jit(solution)/shard_map/pallas_call | solution.py:41
  11.3 0.7 shard_map.85.refs_4_
  12.0 0.6 collective-permute-start.5
  12.7 1.2 %collective-permute-start.4 = (bf16[2,64,1024]{2,1,0:T(8,128)(2,1)S(1)}, bf16[2,64,1024]{2,1,0:T(8,128)(2,1)S(1)}, u32[]{:S(2)}, u32[]{:S(2)}) collective-permute-start(bf16[2,64,1024]{2,1,0:T(8,128)(2,1)S(1)} %get-tuple-element.26), channel_id=1, source_target_pairs={{0,8},{8,16},{16,24},{24,32},{32,40},{40,48},{48,56},{56,64},{64,7... | collective-permute-start | bytes 786440 | tf_op jit(solution)/shard_map/ppermute | solution.py:25
  13.8 0.3 collective-permute-done.1.refs_2_
  14.1 9.8 %collective-permute-done.refs_1_ = bf16[2,64,1024]{2,1,0:T(8,128)(2,1)S(1)} collective-permute-done((bf16[2,64,1024]{2,1,0:T(8,128)(2,1)S(1)}, bf16[2,64,1024]{2,1,0:T(8,128)(2,1)S(1)}, u32[]{:S(2)}, u32[]{:S(2)}) %collective-permute-start) | collective-permute-done | bytes 262176 | tf_op jit(solution)/shard_map/ppermute | solution.py:25
  23.9 1.3 %shard_map.86 = (bf16[2,64,1024]{2,1,0:T(8,128)(2,1)S(1)}, bf16[128,2048]{1,0:T(8,128)(2,1)S(1)}) custom-call(s32[5]{0:T(128)S(1)} %stack.35.flags, bf16[2,128,1024]{2,1,0:T(8,128)(2,1)S(1)} %bitcast.31, bf16[2,64,1024]{2,1,0:T(8,128)(2,1)S(1)} %collective-permute-done.refs_1_, bf16[2,64,1024]{2,1,0:T(8,128)(2,1)S(1)} %collective-permute-done.1.refs_2_, ...), custom_call_target="tpu_custom_call" | custom-call | flops 536870912 | bytes 1048576 | tf_op jit(solution)/shard_map/pallas_call | solution.py:41
  25.2 0.7 shard_map.87.refs_4_
  25.9 0.0 collective-permute-start.3
  26.0 0.0 copy-start.6
  26.0 0.0 copy-start.7
  26.0 0.1 collective-permute-start.2
  26.1 0.0 collective-permute-done.5.refs_2_
  26.1 3.2 %collective-permute-done.4.refs_1_ = bf16[2,64,1024]{2,1,0:T(8,128)(2,1)S(1)} collective-permute-done((bf16[2,64,1024]{2,1,0:T(8,128)(2,1)S(1)}, bf16[2,64,1024]{2,1,0:T(8,128)(2,1)S(1)}, u32[]{:S(2)}, u32[]{:S(2)}) %collective-permute-start.4) | collective-permute-done | bytes 262176 | tf_op jit(solution)/shard_map/ppermute | solution.py:25
  29.3 1.3 %shard_map.88 = (bf16[2,64,1024]{2,1,0:T(8,128)(2,1)S(1)}, bf16[128,2048]{1,0:T(8,128)(2,1)S(1)}) custom-call(s32[5]{0:T(128)S(1)} %stack.35.flags, bf16[2,128,1024]{2,1,0:T(8,128)(2,1)S(1)} %bitcast.32, bf16[2,64,1024]{2,1,0:T(8,128)(2,1)S(1)} %collective-permute-done.4.refs_1_, bf16[2,64,1024]{2,1,0:T(8,128)(2,1)S(1)} %collective-permute-done.5.refs_2_, ...), custom_call_target="tpu_custom_call" | custom-call | flops 536870912 | bytes 1048576 | tf_op jit(solution)/shard_map/pallas_call | solution.py:41
  30.6 0.7 shard_map.89._
  31.4 0.0 collective-permute-start.9
  31.4 0.1 collective-permute-start.8
  31.5 1.1 %shard_map.90.refs_4_.table = bf16[2,1024,1024]{2,1,0:T(8,128)(2,1)S(1)} custom-call(f32[2,32,1024]{2,1,0:T(8,128)S(1)} %copy-done.6, f32[2,32,1024]{2,1,0:T(8,128)S(1)} %copy-done.7, bf16[2,64,1024]{2,1,0:T(8,128)(2,1)S(1)} %shard_map.89._), custom_call_target="tpu_custom_call" | custom-call | flops 536870912 | bytes 1048576 | tf_op jit(solution)/shard_map/pallas_call | solution.py:41
  32.6 0.0 collective-permute-done.3.refs_2_
  32.6 4.8 %collective-permute-done.2.refs_1_ = bf16[2,64,1024]{2,1,0:T(8,128)(2,1)S(1)} collective-permute-done((bf16[2,64,1024]{2,1,0:T(8,128)(2,1)S(1)}, bf16[2,64,1024]{2,1,0:T(8,128)(2,1)S(1)}, u32[]{:S(2)}, u32[]{:S(2)}) %collective-permute-start.2) | collective-permute-done | bytes 262176 | tf_op jit(solution)/shard_map/ppermute | solution.py:25
  37.4 1.3 %shard_map.91 = (bf16[2,64,1024]{2,1,0:T(8,128)(2,1)S(1)}, bf16[128,2048]{1,0:T(8,128)(2,1)S(1)}) custom-call(s32[5]{0:T(128)S(1)} %stack.35.flags, bf16[2,128,1024]{2,1,0:T(8,128)(2,1)S(1)} %bitcast.33, bf16[2,64,1024]{2,1,0:T(8,128)(2,1)S(1)} %collective-permute-done.2.refs_1_, bf16[2,64,1024]{2,1,0:T(8,128)(2,1)S(1)} %collective-permute-done.3.refs_2_, ...), custom_call_target="tpu_custom_call" | custom-call | flops 536870912 | bytes 1048576 | tf_op jit(solution)/shard_map/pallas_call | solution.py:41
  38.7 0.7 shard_map.92.refs_4_
  39.4 0.0 collective-permute-start.7
  39.4 0.3 collective-permute-start.6
  39.7 0.0 collective-permute-done.9.refs_2_
  39.7 3.2 %collective-permute-done.8.refs_1_ = bf16[2,64,1024]{2,1,0:T(8,128)(2,1)S(1)} collective-permute-done((bf16[2,64,1024]{2,1,0:T(8,128)(2,1)S(1)}, bf16[2,64,1024]{2,1,0:T(8,128)(2,1)S(1)}, u32[]{:S(2)}, u32[]{:S(2)}) %collective-permute-start.8) | collective-permute-done | bytes 262176 | tf_op jit(solution)/shard_map/ppermute | solution.py:25
  42.9 1.3 %shard_map.93 = (bf16[2,64,1024]{2,1,0:T(8,128)(2,1)S(1)}, bf16[128,2048]{1,0:T(8,128)(2,1)S(1)}) custom-call(s32[5]{0:T(128)S(1)} %stack.35.flags, bf16[2,128,1024]{2,1,0:T(8,128)(2,1)S(1)} %bitcast.34, bf16[2,64,1024]{2,1,0:T(8,128)(2,1)S(1)} %collective-permute-done.8.refs_1_, bf16[2,64,1024]{2,1,0:T(8,128)(2,1)S(1)} %collective-permute-done.9.refs_2_, ...), custom_call_target="tpu_custom_call" | custom-call | flops 536870912 | bytes 1048576 | tf_op jit(solution)/shard_map/pallas_call | solution.py:41
  44.3 0.7 shard_map.94.refs_4_
  45.0 0.0 collective-permute-start.15
  45.0 0.1 collective-permute-start.14
  45.1 0.1 collective-permute-done.7.refs_2_
  45.2 6.2 %collective-permute-done.6.refs_1_ = bf16[2,64,1024]{2,1,0:T(8,128)(2,1)S(1)} collective-permute-done((bf16[2,64,1024]{2,1,0:T(8,128)(2,1)S(1)}, bf16[2,64,1024]{2,1,0:T(8,128)(2,1)S(1)}, u32[]{:S(2)}, u32[]{:S(2)}) %collective-permute-start.6) | collective-permute-done | bytes 262176 | tf_op jit(solution)/shard_map/ppermute | solution.py:25
  51.4 1.3 %shard_map.95 = (bf16[2,64,1024]{2,1,0:T(8,128)(2,1)S(1)}, bf16[128,2048]{1,0:T(8,128)(2,1)S(1)}) custom-call(s32[5]{0:T(128)S(1)} %stack.35.flags, bf16[2,128,1024]{2,1,0:T(8,128)(2,1)S(1)} %bitcast.35, bf16[2,64,1024]{2,1,0:T(8,128)(2,1)S(1)} %collective-permute-done.6.refs_1_, bf16[2,64,1024]{2,1,0:T(8,128)(2,1)S(1)} %collective-permute-done.7.refs_2_, ...), custom_call_target="tpu_custom_call" | custom-call | flops 536870912 | bytes 1048576 | tf_op jit(solution)/shard_map/pallas_call | solution.py:41
  52.7 0.7 shard_map.96.refs_4_
  53.5 1.1 %collective-permute-start.11 = (bf16[2,64,1024]{2,1,0:T(8,128)(2,1)S(1)}, bf16[2,64,1024]{2,1,0:T(8,128)(2,1)S(1)}, u32[]{:S(2)}, u32[]{:S(2)}) collective-permute-start(bf16[2,64,1024]{2,1,0:T(8,128)(2,1)S(1)} %shard_map.96.refs_4_), channel_id=1, source_target_pairs={{0,1},{1,2},{2,3},{3,4},{4,5},{5,6},{6,7},{7,0},{8,9},{9,10},{10,1... | collective-permute-start | bytes 786440 | tf_op jit(solution)/shard_map/ppermute | solution.py:25
  54.6 0.6 collective-permute-start.13
  55.2 5.3 %collective-permute-start.12 = (bf16[2,64,1024]{2,1,0:T(8,128)(2,1)S(1)}, bf16[2,64,1024]{2,1,0:T(8,128)(2,1)S(1)}, u32[]{:S(2)}, u32[]{:S(2)}) collective-permute-start(bf16[2,64,1024]{2,1,0:T(8,128)(2,1)S(1)} %get-tuple-element.32), channel_id=1, source_target_pairs={{0,248},{8,0},{16,8},{24,16},{32,24},{40,32},{48,40},{56,48},{64,5... | collective-permute-start | bytes 786440 | tf_op jit(solution)/shard_map/ppermute | solution.py:25
  60.6 0.0 collective-permute-done.14.refs_1_
  60.6 1.3 %shard_map.97 = (bf16[2,64,1024]{2,1,0:T(8,128)(2,1)S(1)}, bf16[128,2048]{1,0:T(8,128)(2,1)S(1)}) custom-call(s32[5]{0:T(128)S(1)} %stack.35.flags, bf16[2,128,1024]{2,1,0:T(8,128)(2,1)S(1)} %bitcast.36, bf16[2,64,1024]{2,1,0:T(8,128)(2,1)S(1)} %collective-permute-done.14.refs_1_, bf16[2,64,1024]{2,1,0:T(8,128)(2,1)S(1)} %collective-permute-done.15.refs_2_, ...), custom_call_target="tpu_custom_call" | custom-call | flops 536870912 | bytes 1048576 | tf_op jit(solution)/shard_map/pallas_call | solution.py:41
  61.9 0.7 shard_map.98._
  62.6 0.3 collective-permute-start.17
  63.0 1.4 %collective-permute-start.19 = (bf16[2,64,1024]{2,1,0:T(8,128)(2,1)S(1)}, bf16[2,64,1024]{2,1,0:T(8,128)(2,1)S(1)}, u32[]{:S(2)}, u32[]{:S(2)}) collective-permute-start(bf16[2,64,1024]{2,1,0:T(8,128)(2,1)S(1)} %shard_map.98._), channel_id=1, source_target_pairs={{0,7},{1,0},{2,1},{3,2},{4,3},{5,4},{6,5},{7,6},{8,15},{9,8},{10,9... | collective-permute-start | bytes 786440 | tf_op jit(solution)/shard_map/ppermute | solution.py:25
  64.4 3.3 %collective-permute-done.10.west = bf16[2,64,1024]{2,1,0:T(8,128)(2,1)S(1)} collective-permute-done((bf16[2,64,1024]{2,1,0:T(8,128)(2,1)S(1)}, bf16[2,64,1024]{2,1,0:T(8,128)(2,1)S(1)}, u32[]{:S(2)}, u32[]{:S(2)}) %collective-permute-start.10) | collective-permute-done | bytes 262176 | tf_op jit(solution)/shard_map/ppermute | solution.py:25
  67.6 2.1 %collective-permute-start.18 = (bf16[2,64,1024]{2,1,0:T(8,128)(2,1)S(1)}, bf16[2,64,1024]{2,1,0:T(8,128)(2,1)S(1)}, u32[]{:S(2)}, u32[]{:S(2)}) collective-permute-start(bf16[2,64,1024]{2,1,0:T(8,128)(2,1)S(1)} %get-tuple-element.36), channel_id=1, source_target_pairs={{0,248},{8,0},{16,8},{24,16},{32,24},{40,32},{48,40},{56,48},{64,5... | collective-permute-start | bytes 786440 | tf_op jit(solution)/shard_map/ppermute | solution.py:25
  69.7 0.0 collective-permute-done.12.east
  69.7 2.1 %shard_map.99._ = bf16[16,8,1024]{2,1,0:T(8,128)(2,1)S(1)} custom-call(s32[5]{0:T(128)S(1)} %stack.35.flags, bf16[2,64,1024]{2,1,0:T(8,128)(2,1)S(1)} %collective-permute-done.10.west, bf16[2,64,1024]{2,1,0:T(8,128)(2,1)S(1)} %collective-permute-done.11.south, bf16[2,64,1024]{2,1,0:T(8,128)(2,1)S(1)} %collective-permute-done.12.east, ...), custom_call_target="tpu_custom_call" | custom-call | flops 1073741824 | bytes 1048576 | tf_op jit(solution)/shard_map/pallas_call | solution.py:41
  71.9 0.0 copy-start.8
  71.9 0.0 copy-start.9
  71.9 0.0 collective-permute-done.17.south
  71.9 3.7 %collective-permute-done.16.west = bf16[2,64,1024]{2,1,0:T(8,128)(2,1)S(1)} collective-permute-done((bf16[2,64,1024]{2,1,0:T(8,128)(2,1)S(1)}, bf16[2,64,1024]{2,1,0:T(8,128)(2,1)S(1)}, u32[]{:S(2)}, u32[]{:S(2)}) %collective-permute-start.16) | collective-permute-done | bytes 262176 | tf_op jit(solution)/shard_map/ppermute | solution.py:25
  75.6 0.3 collective-permute-done.18.east
  75.9 2.1 %shard_map.100 = bf16[16,8,1024]{2,1,0:T(8,128)(2,1)S(1)} custom-call(s32[5]{0:T(128)S(1)} %stack.35.flags, bf16[2,64,1024]{2,1,0:T(8,128)(2,1)S(1)} %collective-permute-done.16.west, bf16[2,64,1024]{2,1,0:T(8,128)(2,1)S(1)} %collective-permute-done.17.south, bf16[2,64,1024]{2,1,0:T(8,128)(2,1)S(1)} %collective-permute-done.18.east, ...), custom_call_target="tpu_custom_call" | custom-call | flops 1073741824 | bytes 1048576 | tf_op jit(solution)/shard_map/pallas_call | solution.py:41
  78.1 27.0 %all_to_all.5 = bf16[32,8,1024]{2,1,0:T(8,128)(2,1)S(1)} all-to-all(bf16[32,8,1024]{2,1,0:T(8,128)(2,1)S(1)} %pad_maximum_fusion), channel_id=1, replica_groups=mesh['bx'=32,'by'=8] {'bx'}, dimensions={0} | all-to-all | bytes 1048576 | tf_op jit(solution)/shard_map/all_to_all | solution.py:216
  105.1 1.3 %shard_map.101 = f32[256,1024]{1,0:T(8,128)} custom-call(bf16[256,256]{1,0:T(8,128)(2,1)S(1)} %copy-done.8, f32[256,1]{1,0:T(8,128)S(1)} %copy-done.9, bf16[256,1024]{1,0:T(8,128)(2,1)S(1)} %bitcast.37), custom_call_target="tpu_custom_call" | custom-call | flops 134217728 | bytes 1048576 | tf_op jit(solution)/shard_map/pallas_call | solution.py:41
  (19 shorter events, 0.1 us)
Async XLA Ops:
  0.7 2.2 %copy-start = (bf16[1,1,2,1024,1024]{4,3,2,1,0:T(8,128)(2,1)S(1)}, bf16[1,1,2,1024,1024]{4,3,2,1,0:T(8,128)(2,1)}, u32[]{:S(2)}) copy-start(bf16[1,1,2,1024,1024]{4,3,2,1,0:T(8,128)(2,1)} %param.10) | copy-start | bytes 12582916
  2.9 1.0 copy-start.4
  4.0 6.0 %copy-start.1 = (bf16[1,1,2,1024,1024]{4,3,2,1,0:T(8,128)(2,1)S(1)}, bf16[1,1,2,1024,1024]{4,3,2,1,0:T(8,128)(2,1)}, u32[]{:S(2)}) copy-start(bf16[1,1,2,1024,1024]{4,3,2,1,0:T(8,128)(2,1)} %param.10) | copy-start | bytes 12582916
  4.0 6.0 %copy-start.5 = (bf16[1,1,2,128,1024]{4,3,2,1,0:T(8,128)(2,1)S(1)}, bf16[1,1,2,128,1024]{4,3,2,1,0:T(8,128)(2,1)}, u32[]{:S(2)}) copy-start(bf16[1,1,2,128,1024]{4,3,2,1,0:T(8,128)(2,1)} %param.8) | copy-start | bytes 1572868
  5.2 2.3 %copy-start.2 = (bf16[1,1,2,1024,1024]{4,3,2,1,0:T(8,128)(2,1)S(1)}, bf16[1,1,2,1024,1024]{4,3,2,1,0:T(8,128)(2,1)}, u32[]{:S(2)}) copy-start(bf16[1,1,2,1024,1024]{4,3,2,1,0:T(8,128)(2,1)} %param.11) | copy-start | bytes 12582916
  7.6 3.7 %copy-start.3 = (bf16[1,1,2,1024,1024]{4,3,2,1,0:T(8,128)(2,1)S(1)}, bf16[1,1,2,1024,1024]{4,3,2,1,0:T(8,128)(2,1)}, u32[]{:S(2)}) copy-start(bf16[1,1,2,1024,1024]{4,3,2,1,0:T(8,128)(2,1)} %param.11) | copy-start | bytes 12582916
  8.3 5.8 %collective-permute-start.1 = (bf16[2,64,1024]{2,1,0:T(8,128)(2,1)S(1)}, bf16[2,64,1024]{2,1,0:T(8,128)(2,1)S(1)}, u32[]{:S(2)}, u32[]{:S(2)}) collective-permute-start(bf16[2,64,1024]{2,1,0:T(8,128)(2,1)S(1)} %shard_map.83.refs_2_), channel_id=1, source_target_pairs={{0,1},{1,2},{2,3},{3,4},{4,5},{5,6},{6,7},{7,0},{8,9},{9,10},{10,1... | collective-permute-start | bytes 786440 | tf_op jit(solution)/shard_map/ppermute | solution.py:25
  8.3 15.5 %collective-permute-start = (bf16[2,64,1024]{2,1,0:T(8,128)(2,1)S(1)}, bf16[2,64,1024]{2,1,0:T(8,128)(2,1)S(1)}, u32[]{:S(2)}, u32[]{:S(2)}) collective-permute-start(bf16[2,64,1024]{2,1,0:T(8,128)(2,1)S(1)} %get-tuple-element.21), channel_id=1, source_target_pairs={{0,8},{8,16},{16,24},{24,32},{32,40},{40,48},{48,56},{56,64},{64,7... | collective-permute-start | bytes 786440 | tf_op jit(solution)/shard_map/ppermute | solution.py:25
  12.0 14.1 %collective-permute-start.5 = (bf16[2,64,1024]{2,1,0:T(8,128)(2,1)S(1)}, bf16[2,64,1024]{2,1,0:T(8,128)(2,1)S(1)}, u32[]{:S(2)}, u32[]{:S(2)}) collective-permute-start(bf16[2,64,1024]{2,1,0:T(8,128)(2,1)S(1)} %shard_map.85.refs_4_), channel_id=1, source_target_pairs={{0,1},{1,2},{2,3},{3,4},{4,5},{5,6},{6,7},{7,0},{8,9},{9,10},{10,1... | collective-permute-start | bytes 786440 | tf_op jit(solution)/shard_map/ppermute | solution.py:25
  12.7 16.7 %collective-permute-start.4 = (bf16[2,64,1024]{2,1,0:T(8,128)(2,1)S(1)}, bf16[2,64,1024]{2,1,0:T(8,128)(2,1)S(1)}, u32[]{:S(2)}, u32[]{:S(2)}) collective-permute-start(bf16[2,64,1024]{2,1,0:T(8,128)(2,1)S(1)} %get-tuple-element.26), channel_id=1, source_target_pairs={{0,8},{8,16},{16,24},{24,32},{32,40},{40,48},{48,56},{56,64},{64,7... | collective-permute-start | bytes 786440 | tf_op jit(solution)/shard_map/ppermute | solution.py:25
  25.9 6.7 %collective-permute-start.3 = (bf16[2,64,1024]{2,1,0:T(8,128)(2,1)S(1)}, bf16[2,64,1024]{2,1,0:T(8,128)(2,1)S(1)}, u32[]{:S(2)}, u32[]{:S(2)}) collective-permute-start(bf16[2,64,1024]{2,1,0:T(8,128)(2,1)S(1)} %shard_map.87.refs_4_), channel_id=1, source_target_pairs={{0,1},{1,2},{2,3},{3,4},{4,5},{5,6},{6,7},{7,0},{8,9},{9,10},{10,1... | collective-permute-start | bytes 786440 | tf_op jit(solution)/shard_map/ppermute | solution.py:25
  26.0 5.5 %copy-start.6 = (f32[2,32,1024]{2,1,0:T(8,128)S(1)}, f32[2,32,1024]{2,1,0:T(8,128)}, u32[]{:S(2)}) copy-start(f32[2,32,1024]{2,1,0:T(8,128)} %constant.23.clone.coarse) | copy-start | bytes 786436
  26.0 5.5 %copy-start.7 = (f32[2,32,1024]{2,1,0:T(8,128)S(1)}, f32[2,32,1024]{2,1,0:T(8,128)}, u32[]{:S(2)}) copy-start(f32[2,32,1024]{2,1,0:T(8,128)} %constant.24.clone.fine) | copy-start | bytes 786436
  26.0 11.4 %collective-permute-start.2 = (bf16[2,64,1024]{2,1,0:T(8,128)(2,1)S(1)}, bf16[2,64,1024]{2,1,0:T(8,128)(2,1)S(1)}, u32[]{:S(2)}, u32[]{:S(2)}) collective-permute-start(bf16[2,64,1024]{2,1,0:T(8,128)(2,1)S(1)} %get-tuple-element.24), channel_id=1, source_target_pairs={{0,8},{8,16},{16,24},{24,32},{32,40},{40,48},{48,56},{56,64},{64,7... | collective-permute-start | bytes 786440 | tf_op jit(solution)/shard_map/ppermute | solution.py:25
  31.4 8.3 %collective-permute-start.9 = (bf16[2,64,1024]{2,1,0:T(8,128)(2,1)S(1)}, bf16[2,64,1024]{2,1,0:T(8,128)(2,1)S(1)}, u32[]{:S(2)}, u32[]{:S(2)}) collective-permute-start(bf16[2,64,1024]{2,1,0:T(8,128)(2,1)S(1)} %shard_map.89._), channel_id=1, source_target_pairs={{0,1},{1,2},{2,3},{3,4},{4,5},{5,6},{6,7},{7,0},{8,9},{9,10},{10,1... | collective-permute-start | bytes 786440 | tf_op jit(solution)/shard_map/ppermute | solution.py:25
  31.4 11.6 %collective-permute-start.8 = (bf16[2,64,1024]{2,1,0:T(8,128)(2,1)S(1)}, bf16[2,64,1024]{2,1,0:T(8,128)(2,1)S(1)}, u32[]{:S(2)}, u32[]{:S(2)}) collective-permute-start(bf16[2,64,1024]{2,1,0:T(8,128)(2,1)S(1)} %get-tuple-element.30), channel_id=1, source_target_pairs={{0,8},{8,16},{16,24},{24,32},{32,40},{40,48},{48,56},{56,64},{64,7... | collective-permute-start | bytes 786440 | tf_op jit(solution)/shard_map/ppermute | solution.py:25
  39.4 5.8 %collective-permute-start.7 = (bf16[2,64,1024]{2,1,0:T(8,128)(2,1)S(1)}, bf16[2,64,1024]{2,1,0:T(8,128)(2,1)S(1)}, u32[]{:S(2)}, u32[]{:S(2)}) collective-permute-start(bf16[2,64,1024]{2,1,0:T(8,128)(2,1)S(1)} %shard_map.92.refs_4_), channel_id=1, source_target_pairs={{0,1},{1,2},{2,3},{3,4},{4,5},{5,6},{6,7},{7,0},{8,9},{9,10},{10,1... | collective-permute-start | bytes 786440 | tf_op jit(solution)/shard_map/ppermute | solution.py:25
  39.4 12.0 %collective-permute-start.6 = (bf16[2,64,1024]{2,1,0:T(8,128)(2,1)S(1)}, bf16[2,64,1024]{2,1,0:T(8,128)(2,1)S(1)}, u32[]{:S(2)}, u32[]{:S(2)}) collective-permute-start(bf16[2,64,1024]{2,1,0:T(8,128)(2,1)S(1)} %get-tuple-element.28), channel_id=1, source_target_pairs={{0,8},{8,16},{16,24},{24,32},{32,40},{40,48},{48,56},{56,64},{64,7... | collective-permute-start | bytes 786440 | tf_op jit(solution)/shard_map/ppermute | solution.py:25
  45.0 10.2 %collective-permute-start.15 = (bf16[2,64,1024]{2,1,0:T(8,128)(2,1)S(1)}, bf16[2,64,1024]{2,1,0:T(8,128)(2,1)S(1)}, u32[]{:S(2)}, u32[]{:S(2)}) collective-permute-start(bf16[2,64,1024]{2,1,0:T(8,128)(2,1)S(1)} %shard_map.94.refs_4_), channel_id=1, source_target_pairs={{0,1},{1,2},{2,3},{3,4},{4,5},{5,6},{6,7},{7,0},{8,9},{9,10},{10,1... | collective-permute-start | bytes 786440 | tf_op jit(solution)/shard_map/ppermute | solution.py:25
  45.0 15.5 %collective-permute-start.14 = (bf16[2,64,1024]{2,1,0:T(8,128)(2,1)S(1)}, bf16[2,64,1024]{2,1,0:T(8,128)(2,1)S(1)}, u32[]{:S(2)}, u32[]{:S(2)}) collective-permute-start(bf16[2,64,1024]{2,1,0:T(8,128)(2,1)S(1)} %get-tuple-element.34), channel_id=1, source_target_pairs={{0,8},{8,16},{16,24},{24,32},{32,40},{40,48},{48,56},{56,64},{64,7... | collective-permute-start | bytes 786440 | tf_op jit(solution)/shard_map/ppermute | solution.py:25
  53.5 9.5 %collective-permute-start.11 = (bf16[2,64,1024]{2,1,0:T(8,128)(2,1)S(1)}, bf16[2,64,1024]{2,1,0:T(8,128)(2,1)S(1)}, u32[]{:S(2)}, u32[]{:S(2)}) collective-permute-start(bf16[2,64,1024]{2,1,0:T(8,128)(2,1)S(1)} %shard_map.96.refs_4_), channel_id=1, source_target_pairs={{0,1},{1,2},{2,3},{3,4},{4,5},{5,6},{6,7},{7,0},{8,9},{9,10},{10,1... | collective-permute-start | bytes 786440 | tf_op jit(solution)/shard_map/ppermute | solution.py:25
  54.6 9.8 %collective-permute-start.13 = (bf16[2,64,1024]{2,1,0:T(8,128)(2,1)S(1)}, bf16[2,64,1024]{2,1,0:T(8,128)(2,1)S(1)}, u32[]{:S(2)}, u32[]{:S(2)}) collective-permute-start(bf16[2,64,1024]{2,1,0:T(8,128)(2,1)S(1)} %shard_map.96.refs_4_), channel_id=1, source_target_pairs={{0,7},{1,0},{2,1},{3,2},{4,3},{5,4},{6,5},{7,6},{8,15},{9,8},{10,9... | collective-permute-start | bytes 786440 | tf_op jit(solution)/shard_map/ppermute | solution.py:25
  55.2 12.4 %collective-permute-start.10 = (bf16[2,64,1024]{2,1,0:T(8,128)(2,1)S(1)}, bf16[2,64,1024]{2,1,0:T(8,128)(2,1)S(1)}, u32[]{:S(2)}, u32[]{:S(2)}) collective-permute-start(bf16[2,64,1024]{2,1,0:T(8,128)(2,1)S(1)} %get-tuple-element.32), channel_id=1, source_target_pairs={{0,8},{8,16},{16,24},{24,32},{32,40},{40,48},{48,56},{56,64},{64,7... | collective-permute-start | bytes 786440 | tf_op jit(solution)/shard_map/ppermute | solution.py:25
  55.2 14.5 %collective-permute-start.12 = (bf16[2,64,1024]{2,1,0:T(8,128)(2,1)S(1)}, bf16[2,64,1024]{2,1,0:T(8,128)(2,1)S(1)}, u32[]{:S(2)}, u32[]{:S(2)}) collective-permute-start(bf16[2,64,1024]{2,1,0:T(8,128)(2,1)S(1)} %get-tuple-element.32), channel_id=1, source_target_pairs={{0,248},{8,0},{16,8},{24,16},{32,24},{40,32},{48,40},{56,48},{64,5... | collective-permute-start | bytes 786440 | tf_op jit(solution)/shard_map/ppermute | solution.py:25
  62.6 9.3 %collective-permute-start.17 = (bf16[2,64,1024]{2,1,0:T(8,128)(2,1)S(1)}, bf16[2,64,1024]{2,1,0:T(8,128)(2,1)S(1)}, u32[]{:S(2)}, u32[]{:S(2)}) collective-permute-start(bf16[2,64,1024]{2,1,0:T(8,128)(2,1)S(1)} %shard_map.98._), channel_id=1, source_target_pairs={{0,1},{1,2},{2,3},{3,4},{4,5},{5,6},{6,7},{7,0},{8,9},{9,10},{10,1... | collective-permute-start | bytes 786440 | tf_op jit(solution)/shard_map/ppermute | solution.py:25
  63.0 8.9 %collective-permute-start.19 = (bf16[2,64,1024]{2,1,0:T(8,128)(2,1)S(1)}, bf16[2,64,1024]{2,1,0:T(8,128)(2,1)S(1)}, u32[]{:S(2)}, u32[]{:S(2)}) collective-permute-start(bf16[2,64,1024]{2,1,0:T(8,128)(2,1)S(1)} %shard_map.98._), channel_id=1, source_target_pairs={{0,7},{1,0},{2,1},{3,2},{4,3},{5,4},{6,5},{7,6},{8,15},{9,8},{10,9... | collective-permute-start | bytes 786440 | tf_op jit(solution)/shard_map/ppermute | solution.py:25
  64.4 11.3 %collective-permute-start.16 = (bf16[2,64,1024]{2,1,0:T(8,128)(2,1)S(1)}, bf16[2,64,1024]{2,1,0:T(8,128)(2,1)S(1)}, u32[]{:S(2)}, u32[]{:S(2)}) collective-permute-start(bf16[2,64,1024]{2,1,0:T(8,128)(2,1)S(1)} %get-tuple-element.36), channel_id=1, source_target_pairs={{0,8},{8,16},{16,24},{24,32},{32,40},{40,48},{48,56},{56,64},{64,7... | collective-permute-start | bytes 786440 | tf_op jit(solution)/shard_map/ppermute | solution.py:25
  67.6 8.3 %collective-permute-start.18 = (bf16[2,64,1024]{2,1,0:T(8,128)(2,1)S(1)}, bf16[2,64,1024]{2,1,0:T(8,128)(2,1)S(1)}, u32[]{:S(2)}, u32[]{:S(2)}) collective-permute-start(bf16[2,64,1024]{2,1,0:T(8,128)(2,1)S(1)} %get-tuple-element.36), channel_id=1, source_target_pairs={{0,248},{8,0},{16,8},{24,16},{32,24},{40,32},{48,40},{56,48},{64,5... | collective-permute-start | bytes 786440 | tf_op jit(solution)/shard_map/ppermute | solution.py:25
  71.9 33.3 %copy-start.8 = (bf16[256,256]{1,0:T(8,128)(2,1)S(1)}, bf16[256,256]{1,0:T(8,128)(2,1)}, u32[]{:S(2)}) copy-start(bf16[256,256]{1,0:T(8,128)(2,1)} %constant.25.clone.weights) | copy-start | bytes 393220
  71.9 33.3 %copy-start.9 = (f32[256,1]{1,0:T(8,128)S(1)}, f32[256,1]{1,0:T(8,128)}, u32[]{:S(2)}) copy-start(f32[256,1]{1,0:T(8,128)} %constant.26.clone.gain) | copy-start | bytes 3076

commit v3 on v2

v3 whole, which is shorter than its diff:
```python
import functools

import jax
import jax.numpy as jnp
import numpy as np
from jax import lax
from jax.experimental import pallas as pl
from jax.experimental.pallas import tpu as pltpu
from jax.sharding import PartitionSpec as P


F = 1024
TICKS = 4
SHOTS = 128
CUTS = (0, 64, 128)
CHUNKS = len(CUTS) - 1
STEP = 512
TABLE = 1
EAST_FIRST = False
BF16 = jnp.bfloat16
F32 = jnp.float32
MIB = 1 << 20


def shift(value, axis, by):
    n = lax.axis_size(axis)
    return lax.ppermute(value, axis, [(i, (i + by) % n) for i in range(n)])


def swap(value, axis, odd):
    n = lax.axis_size(axis)
    partner = [k ^ 1 if not odd else min(max(((k + 1) ^ 1) - 1, 0), n - 1) for k in range(n)]
    partner = [k if partner[p] != k else p for k, p in enumerate(partner)]
    return lax.ppermute(value, axis, list(enumerate(partner)))


def vmem():
    return pl.BlockSpec(memory_space=pltpu.VMEM)


def anywhere():
    return pl.BlockSpec(memory_space=pl.ANY)


def call(kernel, outs, specs, args, flops, scratch=(), limit=12):
    return pl.pallas_call(
        kernel,
        out_shape=[jax.ShapeDtypeStruct(shape, kind) for shape, kind in outs],
        in_specs=specs,
        out_specs=[vmem() for _ in outs],
        scratch_shapes=list(scratch),
        compiler_params=pltpu.CompilerParams(vmem_limit_bytes=limit * MIB),
        cost_estimate=pl.CostEstimate(flops=flops, bytes_accessed=MIB, transcendentals=0),
    )(*args)


def combine(real, imag, out, lo, hi):
    w = out.shape[1]
    out[0, :, lo:hi] = (real[:w] - imag[w:]).astype(BF16)
    out[1, :, lo:hi] = (imag[:w] + real[w:]).astype(BF16)


def product(pair, operator, out):
    for c in range(0, F, STEP):
        real = jnp.dot(pair[...], operator[0, :, c : c + STEP], preferred_element_type=F32)
        imag = jnp.dot(pair[...], operator[1, :, c : c + STEP], preferred_element_type=F32)
        combine(real, imag, out, c, c + STEP)


def fill(pair, rows):
    w = pair.shape[0] // 2
    for part in range(2):
        for r in range(0, w, 16):
            pair[part * w + r : part * w + r + 16] = rows(part, r).astype(BF16)


FROM_WEST, FROM_SOUTH, FAR_X, FAR_Y, SIGN_X, SIGN_Y = range(TICKS, TICKS + 6)


def row(masks, k):
    return masks[k : k + 1]


def open_kernel(masks, src, *pairs):
    for lo, pair in zip(CUTS, pairs):
        fill(pair, lambda c, r: row(masks, 0) * src[c, lo + r : lo + r + 16].astype(F32))


def east_kernel(tick, lo, masks, src, west, south, op, *rest):
    out, pair = rest[-2:]

    def rows(c, r):
        at = pl.ds(r, 16)
        return (
            row(masks, FROM_WEST) * west[c, at].astype(F32)
            + row(masks, FROM_SOUTH) * south[c, at].astype(F32)
            + row(masks, tick) * src[c, lo + r : lo + r + 16].astype(F32)
        )

    fill(pair, rows)
    product(pair, op, out)


def product_kernel(pair, op, *rest):
    product(pair, op, rest[-1])


def table_kernel(coarse, fine, _, out):
    for a in range(32):
        ca, sa = coarse[0, a : a + 1, :], coarse[1, a : a + 1, :]
        cb, sb = fine[0], fine[1]
        out[0, 32 * a : 32 * a + 32, :] = (ca * cb - sa * sb).astype(BF16)
        out[1, 32 * a : 32 * a + 32, :] = (sa * cb + ca * sb).astype(BF16)


def mirror_kernel(masks, east1, east2, north1, north2, op, table, _, out, pair, refl):
    def rows(c, r):
        at = pl.ds(r, 16)
        along_x = east1[c, at].astype(F32) - row(masks, FAR_X) * east2[c, at].astype(F32)
        along_y = north1[c, at].astype(F32) - row(masks, FAR_Y) * north2[c, at].astype(F32)
        return row(masks, SIGN_X) * along_x + row(masks, SIGN_Y) * along_y

    fill(pair, rows)
    product(pair, op, refl)
    w = refl.shape[1]
    pair[:w] = refl[0]
    pair[w:] = refl[1]
    for c in range(0, F, STEP):
        cos = jnp.dot(pair[...], table[0, :, c : c + STEP], preferred_element_type=F32)
        sin = jnp.dot(pair[...], table[1, :, c : c + STEP], preferred_element_type=F32)
        combine(cos, -sin, refl, c, c + STEP)
    r = lax.broadcasted_iota(jnp.int32, (2 * w, 2 * w), 0)
    k = lax.broadcasted_iota(jnp.int32, (2 * w, 2 * w), 1)
    from_row = (r % 8) // 4 * w + r // 8 * 4 + r % 4
    pick = jnp.where(k == from_row, 1.0, 0.0).astype(BF16)
    for c in range(0, F, STEP):
        rows = jnp.concatenate([refl[0, :, c : c + STEP], refl[1, :, c : c + STEP]], axis=0)
        moved = jnp.dot(pick, rows, preferred_element_type=F32).astype(BF16)
        out[:, :, c : c + STEP] = moved.reshape(w // 4, 8, STEP)


def last_kernel(weights, gain, got, out):
    out[...] = jnp.dot(weights[...], got[...], preferred_element_type=F32) * gain[...]


def line_parts():
    k = np.arange(F, dtype=np.int64)[None, :]
    a = np.arange(32, dtype=np.int64)[:, None]
    coarse = 2.0 * np.pi / F * (a * 32 * k % F)
    fine = 2.0 * np.pi / F * (a * k % F)
    pack = lambda t: jnp.asarray(np.stack([np.cos(t), np.sin(t)]).astype(np.float32))
    return pack(coarse), pack(fine)


def line_weights(blocks, owned):
    u = 2.0 * np.pi * (np.outer(np.arange(blocks), np.arange(blocks)) % blocks) / blocks
    cos = np.cos(u).astype(np.float32)
    sin = np.sin(u).astype(np.float32)
    w = np.zeros((owned, 2, blocks, blocks, 2, owned), np.float32)
    for s in range(owned):
        w[s, 0, :, :, 0, s] = cos.T
        w[s, 0, :, :, 1, s] = sin.T
        w[s, 1, :, :, 1, s] = cos.T
        w[s, 1, :, :, 0, s] = -sin.T
    m = np.where(np.arange(blocks) < blocks // 2, np.arange(blocks), np.arange(blocks) - blocks)
    g = 0.5 * (1.0 + m / np.sqrt(m * m + 1.0))
    n = owned * 2 * blocks
    gain = np.broadcast_to(g[None, None, :, None], (owned, 2, blocks, F)).reshape(n, F)[:, :1]
    return jnp.asarray(w.reshape(n, n), BF16), jnp.asarray(gain, F32)


def shards(source, start_tick, op_x, op_y):
    nx, ny = lax.axis_size("bx"), lax.axis_size("by")
    i, j = lax.axis_index("bx"), lax.axis_index("by")
    src, x_op, y_op = source[0, 0], op_x[0, 0], op_y[0, 0]
    first = start_tick[0, 0]
    flags = jnp.stack(
        [(first <= tick).astype(jnp.int32) for tick in range(TICKS)]
        + [
            (i > 0).astype(jnp.int32),
            (j > 0).astype(jnp.int32),
            ((i > 0) & (i < nx - 1)).astype(jnp.int32),
            ((j > 0) & (j < ny - 1)).astype(jnp.int32),
            2 * (i & 1) - 1,
            2 * (j & 1) - 1,
        ]
        + [jnp.int32(0)] * 6
    )
    masks = jnp.broadcast_to(flags.astype(F32)[:, None], (16, F))
    coarse, fine = line_parts()
    west, south, ahead, above = ([None] * CHUNKS for _ in range(4))
    last = start_tick
    table = None
    sizes = []
    for lo, hi in zip(CUTS[:-1], CUTS[1:]):
        w = hi - lo
        sizes.append((w, ((2, w, F), BF16), ((2 * w, F), BF16), 2 * (2 * w) * (2 * F) * F))
    square = ((2, F, F), BF16)
    opened = call(open_kernel, [size[2] for size in sizes], [vmem(), vmem()], [masks, src], 1 << 20)
    for tick in range(TICKS):
        final = tick == TICKS - 1
        order = [(c, side) for c in range(CHUNKS) for side in (0, 1)]
        if final and EAST_FIRST:
            order = [(c, side) for side in (0, 1) for c in range(CHUNKS)]
        pairs = list(opened)
        for c, side in order:
            w, trace, paired, flops = sizes[c]
            held = [table] if tick > TABLE else []
            if final and side:
                held.append(x_op)
            held_specs = [vmem()] * len(held) + [anywhere()]
            held.append(last)
            if side == 0:
                if tick == 0:
                    (last,) = call(
                        product_kernel, [trace], [vmem()] * 2 + held_specs, [pairs[c], x_op] + held, flops
                    )
                else:
                    body = functools.partial(east_kernel, tick, CUTS[c])
                    args = [masks, src, west[c], south[c], x_op] + held
                    specs = [vmem()] * 5 + held_specs
                    last, pairs[c] = call(body, [trace, paired], specs, args, flops)
                west[c] = swap(last, "bx", True) if final else shift(last, "bx", 1)
                if final:
                    ahead[c] = swap(last, "bx", False)
            else:
                (last,) = call(
                    product_kernel, [trace], [vmem()] * 2 + held_specs, [pairs[c], y_op] + held, flops
                )
                south[c] = swap(last, "by", True) if final else shift(last, "by", 1)
                if final:
                    above[c] = swap(last, "by", False)
        if tick == TABLE:
            (table,) = call(
                table_kernel, [square], [vmem(), vmem(), anywhere()], [coarse, fine, last], 1 << 27
            )
            last = table
    owned = SHOTS // nx
    spectra = []
    for c in range(CHUNKS):
        w, trace, paired, flops = sizes[c]
        (piece,) = call(
            mirror_kernel,
            [((w // owned, 2 * owned, F), BF16)],
            [vmem()] * 7 + [anywhere()],
            [masks, ahead[c], west[c], above[c], south[c], x_op, table, last],
            2 * flops,
            [pltpu.VMEM(paired[0], BF16), pltpu.VMEM(trace[0], BF16)],
        )
        spectra.append(piece)
        last = piece
    pieces = jnp.concatenate(spectra, axis=0)
    regrouped = lax.all_to_all(pieces, "bx", split_axis=0, concat_axis=0, tiled=True)
    weights, gain = line_weights(nx, owned)
    n = nx * 2 * owned
    (up,) = call(last_kernel, [((n, F), F32)], [vmem()] * 3, [weights, gain, regrouped.reshape(n, F)], 1 << 27)
    return up.reshape(1, owned, 2, nx, F)


def solution(mesh):
    placed = (
        P("bx", "by", None, None, None),
        P("bx", "by"),
        P("bx", "by", None, None, None),
        P("bx", "by", None, None, None),
    )

    return jax.shard_map(
        shards,
        mesh=mesh,
        in_specs=placed,
        out_specs=P("by", "bx", None, None, None),
        check_vma=False,
    )
```

time: 107 us -> 107 us (level)
  the two profiles are of different devices: /device:TPU:6 before, /device:TPU:2 now
where the time goes in v3:
time: 107 us; the launch traced here: 106 us
  waiting for transfers between devices  33.9 us (32%)
  blocking collectives  30.7 us (29%)
  Pallas kernels  17.4 us (16%)
  starting transfers between devices  17.3 us (16%)
  local copies, waits for them, and re-layouts  5.98 us (6%)
  between operations  1.07 us (1%)
    all_to_all x1, blocking collectives, shards(): lax.all_to_all(pieces, 'bx', split_axis=0, concat_axis=0, tiled=True)  30.7 us
    ppermute x12, waiting for transfers between devices, shift(): return lax.ppermute(value, axis, [(i, (i + by) % n) for i in range(n)])  29.3 us
    pallas_call x21, Pallas kernels, call(): pl.pallas_call(kernel, out_shape=[jax.ShapeDtypeStruct(shape, kind) for s...  17.4 us
    ppermute x8, starting transfers between devices, swap(): return lax.ppermute(value, axis, list(enumerate(partner)))  9.94 us
    ppermute x12, starting transfers between devices, shift(): return lax.ppermute(value, axis, [(i, (i + by) % n) for i in range(n)])  7.4 us
    unnamed x20, local copies, waits for them, and re-layouts  5.81 us
    ppermute x8, waiting for transfers between devices, swap(): return lax.ppermute(value, axis, list(enumerate(partner)))  4.64 us
  transfers between devices with their start and end apart: 20, of which 9 were waited for; matrix products, arithmetic and copies ran while one was open for 0% of the time, Pallas kernels for 12%

profile of v3, /device:TPU:2, one launch (start us, length us, event | category | flops | bytes accessed | tf_op | source)
XLA Modules:
  0.0 106.4 jit_solution(10526887006239395467)
XLA Ops:
  0.7 0.1 stack.73
  0.8 0.1 broadcast_in_dim.2.masks
  0.9 1.0 copy-done.4
  1.9 0.1 shard_map.82
  2.0 0.0 copy-start
  2.0 2.2 %copy-done = bf16[1,1,2,1024,1024]{4,3,2,1,0:T(8,128)(2,1)S(1)} copy-done((bf16[1,1,2,1024,1024]{4,3,2,1,0:T(8,128)(2,1)S(1)}, bf16[1,1,2,1024,1024]{4,3,2,1,0:T(8,128)(2,1)}, u32[]{:S(2)}) %copy-start) | copy-done | bytes 4194328
  4.2 0.7 shard_map.83.rest_0_
  4.9 0.0 copy-start.2
  4.9 2.5 %copy-done.2 = bf16[1,1,2,1024,1024]{4,3,2,1,0:T(8,128)(2,1)S(1)} copy-done((bf16[1,1,2,1024,1024]{4,3,2,1,0:T(8,128)(2,1)S(1)}, bf16[1,1,2,1024,1024]{4,3,2,1,0:T(8,128)(2,1)}, u32[]{:S(2)}) %copy-start.2) | copy-done | bytes 4194328
  7.5 0.7 shard_map.84.rest_0_
  8.2 0.0 collective-permute-start.1
  8.2 1.7 %collective-permute-start = (bf16[2,64,1024]{2,1,0:T(8,128)(2,1)S(1)}, bf16[2,64,1024]{2,1,0:T(8,128)(2,1)S(1)}, u32[]{:S(2)}, u32[]{:S(2)}) collective-permute-start(bf16[2,64,1024]{2,1,0:T(8,128)(2,1)S(1)} %shard_map.83.rest_0_), channel_id=1, source_target_pairs={{0,8},{8,16},{16,24},{24,32},{32,40},{40,48},{48,56},{56,64},{64,7... | collective-permute-start | bytes 786440 | tf_op jit(solution)/shard_map/ppermute | solution.py:27
  9.9 0.7 shard_map.85.rest_0_
  10.6 0.7 shard_map.86.rest_0_
  11.4 1.2 %collective-permute-start.5 = (bf16[2,64,1024]{2,1,0:T(8,128)(2,1)S(1)}, bf16[2,64,1024]{2,1,0:T(8,128)(2,1)S(1)}, u32[]{:S(2)}, u32[]{:S(2)}) collective-permute-start(bf16[2,64,1024]{2,1,0:T(8,128)(2,1)S(1)} %shard_map.86.rest_0_), channel_id=1, source_target_pairs={{0,1},{1,2},{2,3},{3,4},{4,5},{5,6},{6,7},{7,0},{8,9},{9,10},{10,1... | collective-permute-start | bytes 786440 | tf_op jit(solution)/shard_map/ppermute | solution.py:27
  12.6 1.6 %collective-permute-start.4 = (bf16[2,64,1024]{2,1,0:T(8,128)(2,1)S(1)}, bf16[2,64,1024]{2,1,0:T(8,128)(2,1)S(1)}, u32[]{:S(2)}, u32[]{:S(2)}) collective-permute-start(bf16[2,64,1024]{2,1,0:T(8,128)(2,1)S(1)} %shard_map.85.rest_0_), channel_id=1, source_target_pairs={{0,8},{8,16},{16,24},{24,32},{32,40},{40,48},{48,56},{56,64},{64,7... | collective-permute-start | bytes 786440 | tf_op jit(solution)/shard_map/ppermute | solution.py:27
  14.2 8.8 %collective-permute-done.west = bf16[2,64,1024]{2,1,0:T(8,128)(2,1)S(1)} collective-permute-done((bf16[2,64,1024]{2,1,0:T(8,128)(2,1)S(1)}, bf16[2,64,1024]{2,1,0:T(8,128)(2,1)S(1)}, u32[]{:S(2)}, u32[]{:S(2)}) %collective-permute-start) | collective-permute-done | bytes 262176 | tf_op jit(solution)/shard_map/ppermute | solution.py:27
  22.9 0.8 shard_map.87
  23.7 0.7 shard_map.88.rest_0_
  24.4 0.0 copy-start.6
  24.5 0.0 copy-start.7
  24.5 1.8 %collective-permute-start.3 = (bf16[2,64,1024]{2,1,0:T(8,128)(2,1)S(1)}, bf16[2,64,1024]{2,1,0:T(8,128)(2,1)S(1)}, u32[]{:S(2)}, u32[]{:S(2)}) collective-permute-start(bf16[2,64,1024]{2,1,0:T(8,128)(2,1)S(1)} %shard_map.88.rest_0_), channel_id=1, source_target_pairs={{0,1},{1,2},{2,3},{3,4},{4,5},{5,6},{6,7},{7,0},{8,9},{9,10},{10,1... | collective-permute-start | bytes 786440 | tf_op jit(solution)/shard_map/ppermute | solution.py:27
  26.3 0.0 collective-permute-start.2
  26.3 0.0 collective-permute-done.5.south
  26.3 2.3 %collective-permute-done.4.west = bf16[2,64,1024]{2,1,0:T(8,128)(2,1)S(1)} collective-permute-done((bf16[2,64,1024]{2,1,0:T(8,128)(2,1)S(1)}, bf16[2,64,1024]{2,1,0:T(8,128)(2,1)S(1)}, u32[]{:S(2)}, u32[]{:S(2)}) %collective-permute-start.4) | collective-permute-done | bytes 262176 | tf_op jit(solution)/shard_map/ppermute | solution.py:27
  28.6 0.8 shard_map.89
  29.3 0.1 collective-permute-start.8
  29.4 0.7 shard_map.90._
  30.2 0.7 collective-permute-start.9
  30.8 1.1 %shard_map.91.rest_0_.rest_1_.table = bf16[2,1024,1024]{2,1,0:T(8,128)(2,1)S(1)} custom-call(f32[2,32,1024]{2,1,0:T(8,128)S(1)} %copy-done.6, f32[2,32,1024]{2,1,0:T(8,128)S(1)} %copy-done.7, bf16[2,64,1024]{2,1,0:T(8,128)(2,1)S(1)} %shard_map.90._), custom_call_target="tpu_custom_call" | custom-call | flops 134217728 | bytes 1048576 | tf_op jit(solution)/shard_map/pallas_call | solution.py:46
  31.9 0.0 collective-permute-done.3.south
  31.9 6.8 %collective-permute-done.2.west = bf16[2,64,1024]{2,1,0:T(8,128)(2,1)S(1)} collective-permute-done((bf16[2,64,1024]{2,1,0:T(8,128)(2,1)S(1)}, bf16[2,64,1024]{2,1,0:T(8,128)(2,1)S(1)}, u32[]{:S(2)}, u32[]{:S(2)}) %collective-permute-start.2) | collective-permute-done | bytes 262176 | tf_op jit(solution)/shard_map/ppermute | solution.py:27
  38.8 0.8 shard_map.92
  39.5 0.7 shard_map.93.rest_1_
  40.2 0.0 collective-permute-start.7
  40.3 0.3 collective-permute-start.6
  40.6 3.0 %collective-permute-done.8.west = bf16[2,64,1024]{2,1,0:T(8,128)(2,1)S(1)} collective-permute-done((bf16[2,64,1024]{2,1,0:T(8,128)(2,1)S(1)}, bf16[2,64,1024]{2,1,0:T(8,128)(2,1)S(1)}, u32[]{:S(2)}, u32[]{:S(2)}) %collective-permute-start.8) | collective-permute-done | bytes 262176 | tf_op jit(solution)/shard_map/ppermute | solution.py:27
  43.5 0.8 shard_map.94
  44.3 0.7 shard_map.95.rest_1_
  45.0 0.0 collective-permute-start.15
  45.1 0.1 collective-permute-start.14
  45.2 0.9 collective-permute-done.7.south
  46.1 6.9 %collective-permute-done.6.west = bf16[2,64,1024]{2,1,0:T(8,128)(2,1)S(1)} collective-permute-done((bf16[2,64,1024]{2,1,0:T(8,128)(2,1)S(1)}, bf16[2,64,1024]{2,1,0:T(8,128)(2,1)S(1)}, u32[]{:S(2)}, u32[]{:S(2)}) %collective-permute-start.6) | collective-permute-done | bytes 262176 | tf_op jit(solution)/shard_map/ppermute | solution.py:27
  52.9 0.8 shard_map.96
  53.7 0.7 shard_map.97.rest_1_
  54.4 0.4 collective-permute-start.12
  54.8 2.3 %collective-permute-start.13 = (bf16[2,64,1024]{2,1,0:T(8,128)(2,1)S(1)}, bf16[2,64,1024]{2,1,0:T(8,128)(2,1)S(1)}, u32[]{:S(2)}, u32[]{:S(2)}) collective-permute-start(bf16[2,64,1024]{2,1,0:T(8,128)(2,1)S(1)} %shard_map.97.rest_1_), channel_id=1, source_target_pairs={{0,0},{1,2},{2,1},{3,4},{4,3},{5,6},{6,5},{7,7},{8,8},{9,10},{10,9... | collective-permute-start | bytes 786440 | tf_op jit(solution)/shard_map/ppermute | solution.py:34
  57.2 0.1 collective-permute-start.10
  57.3 0.7 collective-permute-start.11
  58.0 0.6 collective-permute-done.14.west
  58.6 0.8 shard_map.98
  59.3 0.7 shard_map.99._
  60.1 0.2 collective-permute-start.18
  60.3 2.5 %collective-permute-start.19 = (bf16[2,64,1024]{2,1,0:T(8,128)(2,1)S(1)}, bf16[2,64,1024]{2,1,0:T(8,128)(2,1)S(1)}, u32[]{:S(2)}, u32[]{:S(2)}) collective-permute-start(bf16[2,64,1024]{2,1,0:T(8,128)(2,1)S(1)} %shard_map.99._), channel_id=1, source_target_pairs={{0,0},{1,2},{2,1},{3,4},{4,3},{5,6},{6,5},{7,7},{8,8},{9,10},{10,9... | collective-permute-start | bytes 786440 | tf_op jit(solution)/shard_map/ppermute | solution.py:34
  62.8 3.0 %collective-permute-start.16 = (bf16[2,64,1024]{2,1,0:T(8,128)(2,1)S(1)}, bf16[2,64,1024]{2,1,0:T(8,128)(2,1)S(1)}, u32[]{:S(2)}, u32[]{:S(2)}) collective-permute-start(bf16[2,64,1024]{2,1,0:T(8,128)(2,1)S(1)} %get-tuple-element.32.rest_2_), channel_id=1, source_target_pairs={{0,8},{8,0},{16,24},{24,16},{32,40},{40,32},{48,56},{56,48},{64,72... | collective-permute-start | bytes 786440 | tf_op jit(solution)/shard_map/ppermute | solution.py:34
  65.9 0.1 collective-permute-done.10.east1
  66.0 0.7 collective-permute-start.17
  66.6 1.6 %shard_map.100._ = bf16[16,8,1024]{2,1,0:T(8,128)(2,1)S(1)} custom-call(f32[16,1024]{1,0:T(8,128)S(1)} %broadcast_in_dim.2.masks, bf16[2,64,1024]{2,1,0:T(8,128)(2,1)S(1)} %collective-permute-done.10.east1, bf16[2,64,1024]{2,1,0:T(8,128)(2,1)S(1)} %collective-permute-done.11.east2, bf16[2,64,1024]{2,1,0:T(8,128)(2,1)S(1)} %collective-permute-done.12.north1, ...), custom_call_target="tpu_custom_call" | custom-call | flops 1073741824 | bytes 1048576 | tf_op jit(solution)/shard_map/pallas_call | solution.py:46
  68.2 0.0 copy-start.8
  68.3 0.0 copy-start.9
  68.3 4.5 %collective-permute-done.16.east1 = bf16[2,64,1024]{2,1,0:T(8,128)(2,1)S(1)} collective-permute-done((bf16[2,64,1024]{2,1,0:T(8,128)(2,1)S(1)}, bf16[2,64,1024]{2,1,0:T(8,128)(2,1)S(1)}, u32[]{:S(2)}, u32[]{:S(2)}) %collective-permute-start.16) | collective-permute-done | bytes 262176 | tf_op jit(solution)/shard_map/ppermute | solution.py:34
  72.8 1.6 %shard_map.101 = bf16[16,8,1024]{2,1,0:T(8,128)(2,1)S(1)} custom-call(f32[16,1024]{1,0:T(8,128)S(1)} %broadcast_in_dim.2.masks, bf16[2,64,1024]{2,1,0:T(8,128)(2,1)S(1)} %collective-permute-done.16.east1, bf16[2,64,1024]{2,1,0:T(8,128)(2,1)S(1)} %collective-permute-done.17.east2, bf16[2,64,1024]{2,1,0:T(8,128)(2,1)S(1)} %collective-permute-done.18.north1, ...), custom_call_target="tpu_custom_call" | custom-call | flops 1073741824 | bytes 1048576 | tf_op jit(solution)/shard_map/pallas_call | solution.py:46
  74.5 30.7 %all_to_all.5 = bf16[32,8,1024]{2,1,0:T(8,128)(2,1)S(1)} all-to-all(bf16[32,8,1024]{2,1,0:T(8,128)(2,1)S(1)} %pad_maximum_fusion), channel_id=1, replica_groups=mesh['bx'=32,'by'=8] {'bx'}, dimensions={0} | all-to-all | bytes 1048576 | tf_op jit(solution)/shard_map/all_to_all | solution.py:253
  105.2 1.3 %shard_map.102 = f32[256,1024]{1,0:T(8,128)} custom-call(bf16[256,256]{1,0:T(8,128)(2,1)S(1)} %copy-done.8, f32[256,1]{1,0:T(8,128)S(1)} %copy-done.9, bf16[256,1024]{1,0:T(8,128)(2,1)S(1)} %bitcast.42), custom_call_target="tpu_custom_call" | custom-call | flops 134217728 | bytes 1048576 | tf_op jit(solution)/shard_map/pallas_call | solution.py:46
  (24 shorter events, 0.1 us)
Async XLA Ops:
  0.9 1.0 copy-start.4
  2.0 2.2 %copy-start = (bf16[1,1,2,1024,1024]{4,3,2,1,0:T(8,128)(2,1)S(1)}, bf16[1,1,2,1024,1024]{4,3,2,1,0:T(8,128)(2,1)}, u32[]{:S(2)}) copy-start(bf16[1,1,2,1024,1024]{4,3,2,1,0:T(8,128)(2,1)} %param.10) | copy-start | bytes 12582916
  4.2 5.7 %copy-start.1 = (bf16[1,1,2,1024,1024]{4,3,2,1,0:T(8,128)(2,1)S(1)}, bf16[1,1,2,1024,1024]{4,3,2,1,0:T(8,128)(2,1)}, u32[]{:S(2)}) copy-start(bf16[1,1,2,1024,1024]{4,3,2,1,0:T(8,128)(2,1)} %param.10) | copy-start | bytes 12582916
  4.9 2.5 %copy-start.2 = (bf16[1,1,2,1024,1024]{4,3,2,1,0:T(8,128)(2,1)S(1)}, bf16[1,1,2,1024,1024]{4,3,2,1,0:T(8,128)(2,1)}, u32[]{:S(2)}) copy-start(bf16[1,1,2,1024,1024]{4,3,2,1,0:T(8,128)(2,1)} %param.11) | copy-start | bytes 12582916
  7.5 3.2 %copy-start.3 = (bf16[1,1,2,1024,1024]{4,3,2,1,0:T(8,128)(2,1)S(1)}, bf16[1,1,2,1024,1024]{4,3,2,1,0:T(8,128)(2,1)}, u32[]{:S(2)}) copy-start(bf16[1,1,2,1024,1024]{4,3,2,1,0:T(8,128)(2,1)} %param.11) | copy-start | bytes 12582916
  8.2 6.0 %collective-permute-start.1 = (bf16[2,64,1024]{2,1,0:T(8,128)(2,1)S(1)}, bf16[2,64,1024]{2,1,0:T(8,128)(2,1)S(1)}, u32[]{:S(2)}, u32[]{:S(2)}) collective-permute-start(bf16[2,64,1024]{2,1,0:T(8,128)(2,1)S(1)} %shard_map.84.rest_0_), channel_id=1, source_target_pairs={{0,1},{1,2},{2,3},{3,4},{4,5},{5,6},{6,7},{7,0},{8,9},{9,10},{10,1... | collective-permute-start | bytes 786440 | tf_op jit(solution)/shard_map/ppermute | solution.py:27
  8.2 14.7 %collective-permute-start = (bf16[2,64,1024]{2,1,0:T(8,128)(2,1)S(1)}, bf16[2,64,1024]{2,1,0:T(8,128)(2,1)S(1)}, u32[]{:S(2)}, u32[]{:S(2)}) collective-permute-start(bf16[2,64,1024]{2,1,0:T(8,128)(2,1)S(1)} %shard_map.83.rest_0_), channel_id=1, source_target_pairs={{0,8},{8,16},{16,24},{24,32},{32,40},{40,48},{48,56},{56,64},{64,7... | collective-permute-start | bytes 786440 | tf_op jit(solution)/shard_map/ppermute | solution.py:27
  9.9 13.1 %copy-start.5 = (bf16[1,1,2,128,1024]{4,3,2,1,0:T(8,128)(2,1)S(1)}, bf16[1,1,2,128,1024]{4,3,2,1,0:T(8,128)(2,1)}, u32[]{:S(2)}) copy-start(bf16[1,1,2,128,1024]{4,3,2,1,0:T(8,128)(2,1)} %param.8) | copy-start | bytes 1572868
  11.4 14.9 %collective-permute-start.5 = (bf16[2,64,1024]{2,1,0:T(8,128)(2,1)S(1)}, bf16[2,64,1024]{2,1,0:T(8,128)(2,1)S(1)}, u32[]{:S(2)}, u32[]{:S(2)}) collective-permute-start(bf16[2,64,1024]{2,1,0:T(8,128)(2,1)S(1)} %shard_map.86.rest_0_), channel_id=1, source_target_pairs={{0,1},{1,2},{2,3},{3,4},{4,5},{5,6},{6,7},{7,0},{8,9},{9,10},{10,1... | collective-permute-start | bytes 786440 | tf_op jit(solution)/shard_map/ppermute | solution.py:27
  12.6 16.0 %collective-permute-start.4 = (bf16[2,64,1024]{2,1,0:T(8,128)(2,1)S(1)}, bf16[2,64,1024]{2,1,0:T(8,128)(2,1)S(1)}, u32[]{:S(2)}, u32[]{:S(2)}) collective-permute-start(bf16[2,64,1024]{2,1,0:T(8,128)(2,1)S(1)} %shard_map.85.rest_0_), channel_id=1, source_target_pairs={{0,8},{8,16},{16,24},{24,32},{32,40},{40,48},{48,56},{56,64},{64,7... | collective-permute-start | bytes 786440 | tf_op jit(solution)/shard_map/ppermute | solution.py:27
  24.4 6.4 %copy-start.6 = (f32[2,32,1024]{2,1,0:T(8,128)S(1)}, f32[2,32,1024]{2,1,0:T(8,128)}, u32[]{:S(2)}) copy-start(f32[2,32,1024]{2,1,0:T(8,128)} %constant.41.clone.coarse) | copy-start | bytes 786436
  24.5 6.4 %copy-start.7 = (f32[2,32,1024]{2,1,0:T(8,128)S(1)}, f32[2,32,1024]{2,1,0:T(8,128)}, u32[]{:S(2)}) copy-start(f32[2,32,1024]{2,1,0:T(8,128)} %constant.42.clone.fine) | copy-start | bytes 786436
  24.5 7.4 %collective-permute-start.3 = (bf16[2,64,1024]{2,1,0:T(8,128)(2,1)S(1)}, bf16[2,64,1024]{2,1,0:T(8,128)(2,1)S(1)}, u32[]{:S(2)}, u32[]{:S(2)}) collective-permute-start(bf16[2,64,1024]{2,1,0:T(8,128)(2,1)S(1)} %shard_map.88.rest_0_), channel_id=1, source_target_pairs={{0,1},{1,2},{2,3},{3,4},{4,5},{5,6},{6,7},{7,0},{8,9},{9,10},{10,1... | collective-permute-start | bytes 786440 | tf_op jit(solution)/shard_map/ppermute | solution.py:27
  26.3 12.5 %collective-permute-start.2 = (bf16[2,64,1024]{2,1,0:T(8,128)(2,1)S(1)}, bf16[2,64,1024]{2,1,0:T(8,128)(2,1)S(1)}, u32[]{:S(2)}, u32[]{:S(2)}) collective-permute-start(bf16[2,64,1024]{2,1,0:T(8,128)(2,1)S(1)} %get-tuple-element.21.rest_0_), channel_id=1, source_target_pairs={{0,8},{8,16},{16,24},{24,32},{32,40},{40,48},{48,56},{56,64},{64,7... | collective-permute-start | bytes 786440 | tf_op jit(solution)/shard_map/ppermute | solution.py:27
  29.3 14.2 %collective-permute-start.8 = (bf16[2,64,1024]{2,1,0:T(8,128)(2,1)S(1)}, bf16[2,64,1024]{2,1,0:T(8,128)(2,1)S(1)}, u32[]{:S(2)}, u32[]{:S(2)}) collective-permute-start(bf16[2,64,1024]{2,1,0:T(8,128)(2,1)S(1)} %get-tuple-element.24.rest_0_), channel_id=1, source_target_pairs={{0,8},{8,16},{16,24},{24,32},{32,40},{40,48},{48,56},{56,64},{64,7... | collective-permute-start | bytes 786440 | tf_op jit(solution)/shard_map/ppermute | solution.py:27
  30.2 10.4 %collective-permute-start.9 = (bf16[2,64,1024]{2,1,0:T(8,128)(2,1)S(1)}, bf16[2,64,1024]{2,1,0:T(8,128)(2,1)S(1)}, u32[]{:S(2)}, u32[]{:S(2)}) collective-permute-start(bf16[2,64,1024]{2,1,0:T(8,128)(2,1)S(1)} %shard_map.90._), channel_id=1, source_target_pairs={{0,1},{1,2},{2,3},{3,4},{4,5},{5,6},{6,7},{7,0},{8,9},{9,10},{10,1... | collective-permute-start | bytes 786440 | tf_op jit(solution)/shard_map/ppermute | solution.py:27
  40.2 5.8 %collective-permute-start.7 = (bf16[2,64,1024]{2,1,0:T(8,128)(2,1)S(1)}, bf16[2,64,1024]{2,1,0:T(8,128)(2,1)S(1)}, u32[]{:S(2)}, u32[]{:S(2)}) collective-permute-start(bf16[2,64,1024]{2,1,0:T(8,128)(2,1)S(1)} %shard_map.93.rest_1_), channel_id=1, source_target_pairs={{0,1},{1,2},{2,3},{3,4},{4,5},{5,6},{6,7},{7,0},{8,9},{9,10},{10,1... | collective-permute-start | bytes 786440 | tf_op jit(solution)/shard_map/ppermute | solution.py:27
  40.3 12.7 %collective-permute-start.6 = (bf16[2,64,1024]{2,1,0:T(8,128)(2,1)S(1)}, bf16[2,64,1024]{2,1,0:T(8,128)(2,1)S(1)}, u32[]{:S(2)}, u32[]{:S(2)}) collective-permute-start(bf16[2,64,1024]{2,1,0:T(8,128)(2,1)S(1)} %get-tuple-element.25.rest_1_), channel_id=1, source_target_pairs={{0,8},{8,16},{16,24},{24,32},{32,40},{40,48},{48,56},{56,64},{64,7... | collective-permute-start | bytes 786440 | tf_op jit(solution)/shard_map/ppermute | solution.py:27
  45.0 12.2 %collective-permute-start.15 = (bf16[2,64,1024]{2,1,0:T(8,128)(2,1)S(1)}, bf16[2,64,1024]{2,1,0:T(8,128)(2,1)S(1)}, u32[]{:S(2)}, u32[]{:S(2)}) collective-permute-start(bf16[2,64,1024]{2,1,0:T(8,128)(2,1)S(1)} %shard_map.95.rest_1_), channel_id=1, source_target_pairs={{0,1},{1,2},{2,3},{3,4},{4,5},{5,6},{6,7},{7,0},{8,9},{9,10},{10,1... | collective-permute-start | bytes 786440 | tf_op jit(solution)/shard_map/ppermute | solution.py:27
  45.1 13.5 %collective-permute-start.14 = (bf16[2,64,1024]{2,1,0:T(8,128)(2,1)S(1)}, bf16[2,64,1024]{2,1,0:T(8,128)(2,1)S(1)}, u32[]{:S(2)}, u32[]{:S(2)}) collective-permute-start(bf16[2,64,1024]{2,1,0:T(8,128)(2,1)S(1)} %get-tuple-element.28.rest_1_), channel_id=1, source_target_pairs={{0,8},{8,16},{16,24},{24,32},{32,40},{40,48},{48,56},{56,64},{64,7... | collective-permute-start | bytes 786440 | tf_op jit(solution)/shard_map/ppermute | solution.py:27
  54.4 5.8 %collective-permute-start.12 = (bf16[2,64,1024]{2,1,0:T(8,128)(2,1)S(1)}, bf16[2,64,1024]{2,1,0:T(8,128)(2,1)S(1)}, u32[]{:S(2)}, u32[]{:S(2)}) collective-permute-start(bf16[2,64,1024]{2,1,0:T(8,128)(2,1)S(1)} %shard_map.97.rest_1_), channel_id=1, source_target_pairs={{0,1},{1,0},{2,3},{3,2},{4,5},{5,4},{6,7},{7,6},{8,9},{9,8},{10,11... | collective-permute-start | bytes 786440 | tf_op jit(solution)/shard_map/ppermute | solution.py:34
  54.8 8.0 %collective-permute-start.13 = (bf16[2,64,1024]{2,1,0:T(8,128)(2,1)S(1)}, bf16[2,64,1024]{2,1,0:T(8,128)(2,1)S(1)}, u32[]{:S(2)}, u32[]{:S(2)}) collective-permute-start(bf16[2,64,1024]{2,1,0:T(8,128)(2,1)S(1)} %shard_map.97.rest_1_), channel_id=1, source_target_pairs={{0,0},{1,2},{2,1},{3,4},{4,3},{5,6},{6,5},{7,7},{8,8},{9,10},{10,9... | collective-permute-start | bytes 786440 | tf_op jit(solution)/shard_map/ppermute | solution.py:34
  57.2 8.8 %collective-permute-start.10 = (bf16[2,64,1024]{2,1,0:T(8,128)(2,1)S(1)}, bf16[2,64,1024]{2,1,0:T(8,128)(2,1)S(1)}, u32[]{:S(2)}, u32[]{:S(2)}) collective-permute-start(bf16[2,64,1024]{2,1,0:T(8,128)(2,1)S(1)} %get-tuple-element.29.rest_2_), channel_id=1, source_target_pairs={{0,8},{8,0},{16,24},{24,16},{32,40},{40,32},{48,56},{56,48},{64,72... | collective-permute-start | bytes 786440 | tf_op jit(solution)/shard_map/ppermute | solution.py:34
  57.3 9.4 %collective-permute-start.11 = (bf16[2,64,1024]{2,1,0:T(8,128)(2,1)S(1)}, bf16[2,64,1024]{2,1,0:T(8,128)(2,1)S(1)}, u32[]{:S(2)}, u32[]{:S(2)}) collective-permute-start(bf16[2,64,1024]{2,1,0:T(8,128)(2,1)S(1)} %get-tuple-element.29.rest_2_), channel_id=1, source_target_pairs={{0,0},{8,16},{16,8},{24,32},{32,24},{40,48},{48,40},{56,64},{64,56... | collective-permute-start | bytes 786440 | tf_op jit(solution)/shard_map/ppermute | solution.py:34
  60.1 8.2 %collective-permute-start.18 = (bf16[2,64,1024]{2,1,0:T(8,128)(2,1)S(1)}, bf16[2,64,1024]{2,1,0:T(8,128)(2,1)S(1)}, u32[]{:S(2)}, u32[]{:S(2)}) collective-permute-start(bf16[2,64,1024]{2,1,0:T(8,128)(2,1)S(1)} %shard_map.99._), channel_id=1, source_target_pairs={{0,1},{1,0},{2,3},{3,2},{4,5},{5,4},{6,7},{7,6},{8,9},{9,8},{10,11... | collective-permute-start | bytes 786440 | tf_op jit(solution)/shard_map/ppermute | solution.py:34
  60.3 8.0 %collective-permute-start.19 = (bf16[2,64,1024]{2,1,0:T(8,128)(2,1)S(1)}, bf16[2,64,1024]{2,1,0:T(8,128)(2,1)S(1)}, u32[]{:S(2)}, u32[]{:S(2)}) collective-permute-start(bf16[2,64,1024]{2,1,0:T(8,128)(2,1)S(1)} %shard_map.99._), channel_id=1, source_target_pairs={{0,0},{1,2},{2,1},{3,4},{4,3},{5,6},{6,5},{7,7},{8,8},{9,10},{10,9... | collective-permute-start | bytes 786440 | tf_op jit(solution)/shard_map/ppermute | solution.py:34
  62.8 10.0 %collective-permute-start.16 = (bf16[2,64,1024]{2,1,0:T(8,128)(2,1)S(1)}, bf16[2,64,1024]{2,1,0:T(8,128)(2,1)S(1)}, u32[]{:S(2)}, u32[]{:S(2)}) collective-permute-start(bf16[2,64,1024]{2,1,0:T(8,128)(2,1)S(1)} %get-tuple-element.32.rest_2_), channel_id=1, source_target_pairs={{0,8},{8,0},{16,24},{24,16},{32,40},{40,32},{48,56},{56,48},{64,72... | collective-permute-start | bytes 786440 | tf_op jit(solution)/shard_map/ppermute | solution.py:34
  66.0 6.9 %collective-permute-start.17 = (bf16[2,64,1024]{2,1,0:T(8,128)(2,1)S(1)}, bf16[2,64,1024]{2,1,0:T(8,128)(2,1)S(1)}, u32[]{:S(2)}, u32[]{:S(2)}) collective-permute-start(bf16[2,64,1024]{2,1,0:T(8,128)(2,1)S(1)} %get-tuple-element.32.rest_2_), channel_id=1, source_target_pairs={{0,0},{8,16},{16,8},{24,32},{32,24},{40,48},{48,40},{56,64},{64,56... | collective-permute-start | bytes 786440 | tf_op jit(solution)/shard_map/ppermute | solution.py:34
  68.2 36.9 %copy-start.8 = (bf16[256,256]{1,0:T(8,128)(2,1)S(1)}, bf16[256,256]{1,0:T(8,128)(2,1)}, u32[]{:S(2)}) copy-start(bf16[256,256]{1,0:T(8,128)(2,1)} %constant.43.clone.weights) | copy-start | bytes 393220
  68.3 36.9 %copy-start.9 = (f32[256,1]{1,0:T(8,128)S(1)}, f32[256,1]{1,0:T(8,128)}, u32[]{:S(2)}) copy-start(f32[256,1]{1,0:T(8,128)} %constant.44.clone.gain) | copy-start | bytes 3076

commit v4 on v3

--- a/solution.py
+++ b/solution.py
@@ -74,7 +74,7 @@
             pair[part * w + r : part * w + r + 16] = rows(part, r).astype(BF16)
 
 
-FROM_WEST, FROM_SOUTH, FAR_X, FAR_Y, SIGN_X, SIGN_Y = range(TICKS, TICKS + 6)
+FROM_WEST, FROM_SOUTH, FAR_X, FAR_Y, SIGN_X, _ = range(TICKS, TICKS + 6)
 
 
 def row(masks, k):
@@ -113,12 +113,15 @@
         out[1, 32 * a : 32 * a + 32, :] = (sa * cb + ca * sb).astype(BF16)
 
 
-def mirror_kernel(masks, east1, east2, north1, north2, op, table, _, out, pair, refl):
+def mirror_kernel(before, masks, east1, east2, north1, north2, op, table, held, out, pair, refl):
+    if before:
+        out[:before] = held[...]
+
     def rows(c, r):
         at = pl.ds(r, 16)
         along_x = east1[c, at].astype(F32) - row(masks, FAR_X) * east2[c, at].astype(F32)
-        along_y = north1[c, at].astype(F32) - row(masks, FAR_Y) * north2[c, at].astype(F32)
-        return row(masks, SIGN_X) * along_x + row(masks, SIGN_Y) * along_y
+        along_y = row(masks, FROM_SOUTH) * north2[c, at].astype(F32) - row(masks, FAR_Y) * north1[c, at].astype(F32)
+        return row(masks, SIGN_X) * along_x + along_y
 
     fill(pair, rows)
     product(pair, op, refl)
@@ -136,7 +139,7 @@
     for c in range(0, F, STEP):
         rows = jnp.concatenate([refl[0, :, c : c + STEP], refl[1, :, c : c + STEP]], axis=0)
         moved = jnp.dot(pick, rows, preferred_element_type=F32).astype(BF16)
-        out[:, :, c : c + STEP] = moved.reshape(w // 4, 8, STEP)
+        out[before:, :, c : c + STEP] = moved.reshape(w // 4, 8, STEP)
 
 
 def last_kernel(weights, gain, got, out):
@@ -180,7 +183,7 @@
             (i > 0).astype(jnp.int32),
             (j > 0).astype(jnp.int32),
             ((i > 0) & (i < nx - 1)).astype(jnp.int32),
-            ((j > 0) & (j < ny - 1)).astype(jnp.int32),
+            (j < ny - 1).astype(jnp.int32),
             2 * (i & 1) - 1,
             2 * (j & 1) - 1,
         ]
@@ -227,29 +230,27 @@
                 (last,) = call(
                     product_kernel, [trace], [vmem()] * 2 + held_specs, [pairs[c], y_op] + held, flops
                 )
-                south[c] = swap(last, "by", True) if final else shift(last, "by", 1)
+                south[c] = shift(last, "by", 1)
                 if final:
-                    above[c] = swap(last, "by", False)
+                    above[c] = shift(last, "by", -1)
         if tick == TABLE:
             (table,) = call(
                 table_kernel, [square], [vmem(), vmem(), anywhere()], [coarse, fine, last], 1 << 27
             )
             last = table
     owned = SHOTS // nx
-    spectra = []
     for c in range(CHUNKS):
         w, trace, paired, flops = sizes[c]
-        (piece,) = call(
-            mirror_kernel,
-            [((w // owned, 2 * owned, F), BF16)],
-            [vmem()] * 7 + [anywhere()],
+        before = CUTS[c] // owned
+        (last,) = call(
+            functools.partial(mirror_kernel, before),
+            [((before + w // owned, 2 * owned, F), BF16)],
+            [vmem()] * 7 + [vmem() if before else anywhere()],
             [masks, ahead[c], west[c], above[c], south[c], x_op, table, last],
             2 * flops,
             [pltpu.VMEM(paired[0], BF16), pltpu.VMEM(trace[0], BF16)],
         )
-        spectra.append(piece)
-        last = piece
-    pieces = jnp.concatenate(spectra, axis=0)
+    pieces = last
     regrouped = lax.all_to_all(pieces, "bx", split_axis=0, concat_axis=0, tiled=True)
     weights, gain = line_weights(nx, owned)
     n = nx * 2 * owned

time: 107 us -> 104 us (0.972)
  starting transfers between devices: 17.3 us -> 11.4 us
  waiting for transfers between devices: 33.9 us -> 37.1 us
    ppermute x8 -> x4, starting transfers between devices: 9.94 us -> 2.58 us  [swap(): return lax.ppermute(value, axis, list(enumerate(partner)))]
    ppermute x12 -> x16, waiting for transfers between devices: 29.3 us -> 31.5 us  [shift(): return lax.ppermute(value, axis, [(i, (i + by) % n) for i in range(n)])]
    ppermute x12 -> x16, starting transfers between devices: 7.4 us -> 8.84 us  [shift(): return lax.ppermute(value, axis, [(i, (i + by) % n) for i in range(n)])]
    ppermute x8 -> x4, waiting for transfers between devices: 4.64 us -> 5.58 us  [swap(): return lax.ppermute(value, axis, list(enumerate(partner)))]
  transfers between devices with their start and end apart: 20 -> 20, of which waited for: 9 -> 10; matrix products, arithmetic and copies ran while one was open for 0% -> 0% of each run, Pallas kernels for 12% -> 13%
where the time goes in v4:
time: 104 us
  waiting for transfers between devices  37.1 us (36%)
  blocking collectives  30.7 us (30%)
  Pallas kernels  17.5 us (17%)
  starting transfers between devices  11.4 us (11%)
  local copies, waits for them, and re-layouts  5.98 us (6%)
    ppermute x16, waiting for transfers between devices, shift(): return lax.ppermute(value, axis, [(i, (i + by) % n) for i in range(n)])  31.5 us
    all_to_all x1, blocking collectives, shards(): lax.all_to_all(pieces, 'bx', split_axis=0, concat_axis=0, tiled=True)  30.7 us
    pallas_call x21, Pallas kernels, call(): pl.pallas_call(kernel, out_shape=[jax.ShapeDtypeStruct(shape, kind) for s...  17.5 us
    ppermute x16, starting transfers between devices, shift(): return lax.ppermute(value, axis, [(i, (i + by) % n) for i in range(n)])  8.84 us
    unnamed x20, local copies, waits for them, and re-layouts  5.81 us
    ppermute x4, waiting for transfers between devices, swap(): return lax.ppermute(value, axis, list(enumerate(partner)))  5.58 us
    ppermute x4, starting transfers between devices, swap(): return lax.ppermute(value, axis, list(enumerate(partner)))  2.58 us
  transfers between devices with their start and end apart: 20, of which 10 were waited for; matrix products, arithmetic and copies ran while one was open for 0% of the time, Pallas kernels for 13%

profile of v4, /device:TPU:2, one launch (start us, length us, event | category | flops | bytes accessed | tf_op | source)
XLA Modules:
  0.0 103.7 jit_solution(7544520723849341517)
XLA Ops:
  0.7 0.1 stack.73
  0.8 0.1 broadcast_in_dim.2.masks
  0.9 1.0 %copy-done.4 = bf16[1,1,2,128,1024]{4,3,2,1,0:T(8,128)(2,1)S(1)} copy-done((bf16[1,1,2,128,1024]{4,3,2,1,0:T(8,128)(2,1)S(1)}, bf16[1,1,2,128,1024]{4,3,2,1,0:T(8,128)(2,1)}, u32[]{:S(2)}) %copy-start.4) | copy-done | bytes 524312
  1.9 0.1 shard_map.82
  2.0 0.0 copy-start
  2.0 2.2 %copy-done = bf16[1,1,2,1024,1024]{4,3,2,1,0:T(8,128)(2,1)S(1)} copy-done((bf16[1,1,2,1024,1024]{4,3,2,1,0:T(8,128)(2,1)S(1)}, bf16[1,1,2,1024,1024]{4,3,2,1,0:T(8,128)(2,1)}, u32[]{:S(2)}) %copy-start) | copy-done | bytes 4194328
  4.2 0.7 shard_map.83.rest_0_
  4.9 0.0 copy-start.2
  4.9 2.5 %copy-done.2 = bf16[1,1,2,1024,1024]{4,3,2,1,0:T(8,128)(2,1)S(1)} copy-done((bf16[1,1,2,1024,1024]{4,3,2,1,0:T(8,128)(2,1)S(1)}, bf16[1,1,2,1024,1024]{4,3,2,1,0:T(8,128)(2,1)}, u32[]{:S(2)}) %copy-start.2) | copy-done | bytes 4194328
  7.5 0.7 shard_map.84.rest_0_
  8.2 0.0 collective-permute-start.3
  8.2 1.7 %collective-permute-start.2 = (bf16[2,64,1024]{2,1,0:T(8,128)(2,1)S(1)}, bf16[2,64,1024]{2,1,0:T(8,128)(2,1)S(1)}, u32[]{:S(2)}, u32[]{:S(2)}) collective-permute-start(bf16[2,64,1024]{2,1,0:T(8,128)(2,1)S(1)} %shard_map.83.rest_0_), channel_id=1, source_target_pairs={{0,8},{8,16},{16,24},{24,32},{32,40},{40,48},{48,56},{56,64},{64,7... | collective-permute-start | bytes 786440 | tf_op jit(solution)/shard_map/ppermute | solution.py:27
  9.9 0.7 shard_map.85.rest_0_
  10.6 0.7 shard_map.86.rest_0_
  11.4 1.3 %collective-permute-start.1 = (bf16[2,64,1024]{2,1,0:T(8,128)(2,1)S(1)}, bf16[2,64,1024]{2,1,0:T(8,128)(2,1)S(1)}, u32[]{:S(2)}, u32[]{:S(2)}) collective-permute-start(bf16[2,64,1024]{2,1,0:T(8,128)(2,1)S(1)} %shard_map.86.rest_0_), channel_id=1, source_target_pairs={{0,1},{1,2},{2,3},{3,4},{4,5},{5,6},{6,7},{7,0},{8,9},{9,10},{10,1... | collective-permute-start | bytes 786440 | tf_op jit(solution)/shard_map/ppermute | solution.py:27
  12.6 1.6 %collective-permute-start = (bf16[2,64,1024]{2,1,0:T(8,128)(2,1)S(1)}, bf16[2,64,1024]{2,1,0:T(8,128)(2,1)S(1)}, u32[]{:S(2)}, u32[]{:S(2)}) collective-permute-start(bf16[2,64,1024]{2,1,0:T(8,128)(2,1)S(1)} %shard_map.85.rest_0_), channel_id=1, source_target_pairs={{0,8},{8,16},{16,24},{24,32},{32,40},{40,48},{48,56},{56,64},{64,7... | collective-permute-start | bytes 786440 | tf_op jit(solution)/shard_map/ppermute | solution.py:27
  14.2 8.7 %collective-permute-done.2.west = bf16[2,64,1024]{2,1,0:T(8,128)(2,1)S(1)} collective-permute-done((bf16[2,64,1024]{2,1,0:T(8,128)(2,1)S(1)}, bf16[2,64,1024]{2,1,0:T(8,128)(2,1)S(1)}, u32[]{:S(2)}, u32[]{:S(2)}) %collective-permute-start.2) | collective-permute-done | bytes 262176 | tf_op jit(solution)/shard_map/ppermute | solution.py:27
  22.9 0.8 shard_map.87
  23.7 0.7 shard_map.88.rest_0_
  24.4 0.0 copy-start.6
  24.5 0.0 copy-start.7
  24.5 1.8 %collective-permute-start.7 = (bf16[2,64,1024]{2,1,0:T(8,128)(2,1)S(1)}, bf16[2,64,1024]{2,1,0:T(8,128)(2,1)S(1)}, u32[]{:S(2)}, u32[]{:S(2)}) collective-permute-start(bf16[2,64,1024]{2,1,0:T(8,128)(2,1)S(1)} %shard_map.88.rest_0_), channel_id=1, source_target_pairs={{0,1},{1,2},{2,3},{3,4},{4,5},{5,6},{6,7},{7,0},{8,9},{9,10},{10,1... | collective-permute-start | bytes 786440 | tf_op jit(solution)/shard_map/ppermute | solution.py:27
  26.3 0.0 collective-permute-done.1.south
  26.3 2.3 %collective-permute-done.west = bf16[2,64,1024]{2,1,0:T(8,128)(2,1)S(1)} collective-permute-done((bf16[2,64,1024]{2,1,0:T(8,128)(2,1)S(1)}, bf16[2,64,1024]{2,1,0:T(8,128)(2,1)S(1)}, u32[]{:S(2)}, u32[]{:S(2)}) %collective-permute-start) | collective-permute-done | bytes 262176 | tf_op jit(solution)/shard_map/ppermute | solution.py:27
  28.6 0.8 shard_map.89
  29.3 0.1 collective-permute-start.4
  29.4 0.7 shard_map.90._
  30.2 0.7 collective-permute-start.5
  30.8 1.1 %shard_map.91.rest_0_.rest_1_.table = bf16[2,1024,1024]{2,1,0:T(8,128)(2,1)S(1)} custom-call(f32[2,32,1024]{2,1,0:T(8,128)S(1)} %copy-done.6, f32[2,32,1024]{2,1,0:T(8,128)S(1)} %copy-done.7, bf16[2,64,1024]{2,1,0:T(8,128)(2,1)S(1)} %shard_map.90._), custom_call_target="tpu_custom_call" | custom-call | flops 134217728 | bytes 1048576 | tf_op jit(solution)/shard_map/pallas_call | solution.py:46
  31.9 6.8 %collective-permute-done.6.west = bf16[2,64,1024]{2,1,0:T(8,128)(2,1)S(1)} collective-permute-done((bf16[2,64,1024]{2,1,0:T(8,128)(2,1)S(1)}, bf16[2,64,1024]{2,1,0:T(8,128)(2,1)S(1)}, u32[]{:S(2)}, u32[]{:S(2)}) %collective-permute-start.6) | collective-permute-done | bytes 262176 | tf_op jit(solution)/shard_map/ppermute | solution.py:27
  38.8 0.8 shard_map.92
  39.5 0.7 shard_map.93.rest_1_
  40.3 0.0 collective-permute-start.11
  40.3 0.3 collective-permute-start.10
  40.6 3.0 %collective-permute-done.4.west = bf16[2,64,1024]{2,1,0:T(8,128)(2,1)S(1)} collective-permute-done((bf16[2,64,1024]{2,1,0:T(8,128)(2,1)S(1)}, bf16[2,64,1024]{2,1,0:T(8,128)(2,1)S(1)}, u32[]{:S(2)}, u32[]{:S(2)}) %collective-permute-start.4) | collective-permute-done | bytes 262176 | tf_op jit(solution)/shard_map/ppermute | solution.py:27
  43.6 0.8 shard_map.94
  44.3 0.7 shard_map.95.rest_1_
  45.1 0.0 collective-permute-start.9
  45.1 0.1 collective-permute-start.8
  45.2 0.9 collective-permute-done.11.south
  46.1 6.9 %collective-permute-done.10.west = bf16[2,64,1024]{2,1,0:T(8,128)(2,1)S(1)} collective-permute-done((bf16[2,64,1024]{2,1,0:T(8,128)(2,1)S(1)}, bf16[2,64,1024]{2,1,0:T(8,128)(2,1)S(1)}, u32[]{:S(2)}, u32[]{:S(2)}) %collective-permute-start.10) | collective-permute-done | bytes 262176 | tf_op jit(solution)/shard_map/ppermute | solution.py:27
  53.0 0.8 shard_map.96
  53.8 0.7 shard_map.97.rest_1_
  54.5 0.7 collective-permute-start.18
  55.2 0.0 collective-permute-start.19
  55.2 0.0 collective-permute-start.16
  55.2 0.0 collective-permute-done.9.south
  55.2 0.7 collective-permute-start.17
  55.9 2.7 %collective-permute-done.8.west = bf16[2,64,1024]{2,1,0:T(8,128)(2,1)S(1)} collective-permute-done((bf16[2,64,1024]{2,1,0:T(8,128)(2,1)S(1)}, bf16[2,64,1024]{2,1,0:T(8,128)(2,1)S(1)}, u32[]{:S(2)}, u32[]{:S(2)}) %collective-permute-start.8) | collective-permute-done | bytes 262176 | tf_op jit(solution)/shard_map/ppermute | solution.py:27
  58.6 0.8 shard_map.98
  59.4 0.7 shard_map.99.held
  60.1 0.0 collective-permute-start.14
  60.1 0.7 collective-permute-start.15
  60.8 0.1 collective-permute-done.19.north2
  61.0 1.2 %collective-permute-start.12 = (bf16[2,64,1024]{2,1,0:T(8,128)(2,1)S(1)}, bf16[2,64,1024]{2,1,0:T(8,128)(2,1)S(1)}, u32[]{:S(2)}, u32[]{:S(2)}) collective-permute-start(bf16[2,64,1024]{2,1,0:T(8,128)(2,1)S(1)} %get-tuple-element.31.rest_2_), channel_id=1, source_target_pairs={{0,8},{8,0},{16,24},{24,16},{32,40},{40,32},{48,56},{56,48},{64,72... | collective-permute-start | bytes 786440 | tf_op jit(solution)/shard_map/ppermute | solution.py:34
  62.2 1.8 %collective-permute-done.16.east1 = bf16[2,64,1024]{2,1,0:T(8,128)(2,1)S(1)} collective-permute-done((bf16[2,64,1024]{2,1,0:T(8,128)(2,1)S(1)}, bf16[2,64,1024]{2,1,0:T(8,128)(2,1)S(1)}, u32[]{:S(2)}, u32[]{:S(2)}) %collective-permute-start.16) | collective-permute-done | bytes 262176 | tf_op jit(solution)/shard_map/ppermute | solution.py:34
  64.0 0.7 collective-permute-start.13
  64.7 1.6 %shard_map.100.held = bf16[16,8,1024]{2,1,0:T(8,128)(2,1)S(1)} custom-call(f32[16,1024]{1,0:T(8,128)S(1)} %broadcast_in_dim.2.masks, bf16[2,64,1024]{2,1,0:T(8,128)(2,1)S(1)} %collective-permute-done.16.east1, bf16[2,64,1024]{2,1,0:T(8,128)(2,1)S(1)} %collective-permute-done.17.east2, bf16[2,64,1024]{2,1,0:T(8,128)(2,1)S(1)} %collective-permute-done.18.north1, ...), custom_call_target="tpu_custom_call" | custom-call | flops 1073741824 | bytes 1048576 | tf_op jit(solution)/shard_map/pallas_call | solution.py:46
  66.3 0.0 copy-start.8
  66.3 0.0 copy-start.9
  66.4 3.8 %collective-permute-done.12.east1 = bf16[2,64,1024]{2,1,0:T(8,128)(2,1)S(1)} collective-permute-done((bf16[2,64,1024]{2,1,0:T(8,128)(2,1)S(1)}, bf16[2,64,1024]{2,1,0:T(8,128)(2,1)S(1)}, u32[]{:S(2)}, u32[]{:S(2)}) %collective-permute-start.12) | collective-permute-done | bytes 262176 | tf_op jit(solution)/shard_map/ppermute | solution.py:34
  70.1 1.6 %shard_map.101 = bf16[32,8,1024]{2,1,0:T(8,128)(2,1)S(1)} custom-call(f32[16,1024]{1,0:T(8,128)S(1)} %broadcast_in_dim.2.masks, bf16[2,64,1024]{2,1,0:T(8,128)(2,1)S(1)} %collective-permute-done.12.east1, bf16[2,64,1024]{2,1,0:T(8,128)(2,1)S(1)} %collective-permute-done.13.east2, bf16[2,64,1024]{2,1,0:T(8,128)(2,1)S(1)} %collective-permute-done.14.north1, ...), custom_call_target="tpu_custom_call" | custom-call | flops 1073741824 | bytes 1048576 | tf_op jit(solution)/shard_map/pallas_call | solution.py:46
  71.7 30.7 %all_to_all.5 = bf16[32,8,1024]{2,1,0:T(8,128)(2,1)S(1)} all-to-all(bf16[32,8,1024]{2,1,0:T(8,128)(2,1)S(1)} %shard_map.101), channel_id=1, replica_groups=mesh['bx'=32,'by'=8] {'bx'}, dimensions={0} | all-to-all | bytes 1048576 | tf_op jit(solution)/shard_map/all_to_all | solution.py:254
  102.4 1.3 %shard_map.102 = f32[256,1024]{1,0:T(8,128)} custom-call(bf16[256,256]{1,0:T(8,128)(2,1)S(1)} %copy-done.8, f32[256,1]{1,0:T(8,128)S(1)} %copy-done.9, bf16[256,1024]{1,0:T(8,128)(2,1)S(1)} %bitcast.42), custom_call_target="tpu_custom_call" | custom-call | flops 134217728 | bytes 1048576 | tf_op jit(solution)/shard_map/pallas_call | solution.py:46
  (23 shorter events, 0.1 us)
Async XLA Ops:
  0.9 1.0 %copy-start.4 = (bf16[1,1,2,128,1024]{4,3,2,1,0:T(8,128)(2,1)S(1)}, bf16[1,1,2,128,1024]{4,3,2,1,0:T(8,128)(2,1)}, u32[]{:S(2)}) copy-start(bf16[1,1,2,128,1024]{4,3,2,1,0:T(8,128)(2,1)} %param.8) | copy-start | bytes 1572868
  2.0 2.2 %copy-start = (bf16[1,1,2,1024,1024]{4,3,2,1,0:T(8,128)(2,1)S(1)}, bf16[1,1,2,1024,1024]{4,3,2,1,0:T(8,128)(2,1)}, u32[]{:S(2)}) copy-start(bf16[1,1,2,1024,1024]{4,3,2,1,0:T(8,128)(2,1)} %param.10) | copy-start | bytes 12582916
  4.2 5.7 %copy-start.1 = (bf16[1,1,2,1024,1024]{4,3,2,1,0:T(8,128)(2,1)S(1)}, bf16[1,1,2,1024,1024]{4,3,2,1,0:T(8,128)(2,1)}, u32[]{:S(2)}) copy-start(bf16[1,1,2,1024,1024]{4,3,2,1,0:T(8,128)(2,1)} %param.10) | copy-start | bytes 12582916
  4.9 2.5 %copy-start.2 = (bf16[1,1,2,1024,1024]{4,3,2,1,0:T(8,128)(2,1)S(1)}, bf16[1,1,2,1024,1024]{4,3,2,1,0:T(8,128)(2,1)}, u32[]{:S(2)}) copy-start(bf16[1,1,2,1024,1024]{4,3,2,1,0:T(8,128)(2,1)} %param.11) | copy-start | bytes 12582916
  7.5 3.1 %copy-start.3 = (bf16[1,1,2,1024,1024]{4,3,2,1,0:T(8,128)(2,1)S(1)}, bf16[1,1,2,1024,1024]{4,3,2,1,0:T(8,128)(2,1)}, u32[]{:S(2)}) copy-start(bf16[1,1,2,1024,1024]{4,3,2,1,0:T(8,128)(2,1)} %param.11) | copy-start | bytes 12582916
  8.2 6.0 %collective-permute-start.3 = (bf16[2,64,1024]{2,1,0:T(8,128)(2,1)S(1)}, bf16[2,64,1024]{2,1,0:T(8,128)(2,1)S(1)}, u32[]{:S(2)}, u32[]{:S(2)}) collective-permute-start(bf16[2,64,1024]{2,1,0:T(8,128)(2,1)S(1)} %shard_map.84.rest_0_), channel_id=1, source_target_pairs={{0,1},{1,2},{2,3},{3,4},{4,5},{5,6},{6,7},{7,0},{8,9},{9,10},{10,1... | collective-permute-start | bytes 786440 | tf_op jit(solution)/shard_map/ppermute | solution.py:27
  8.2 14.7 %collective-permute-start.2 = (bf16[2,64,1024]{2,1,0:T(8,128)(2,1)S(1)}, bf16[2,64,1024]{2,1,0:T(8,128)(2,1)S(1)}, u32[]{:S(2)}, u32[]{:S(2)}) collective-permute-start(bf16[2,64,1024]{2,1,0:T(8,128)(2,1)S(1)} %shard_map.83.rest_0_), channel_id=1, source_target_pairs={{0,8},{8,16},{16,24},{24,32},{32,40},{40,48},{48,56},{56,64},{64,7... | collective-permute-start | bytes 786440 | tf_op jit(solution)/shard_map/ppermute | solution.py:27
  9.9 13.1 %copy-start.5 = (bf16[1,1,2,128,1024]{4,3,2,1,0:T(8,128)(2,1)S(1)}, bf16[1,1,2,128,1024]{4,3,2,1,0:T(8,128)(2,1)}, u32[]{:S(2)}) copy-start(bf16[1,1,2,128,1024]{4,3,2,1,0:T(8,128)(2,1)} %param.8) | copy-start | bytes 1572868
  11.4 14.9 %collective-permute-start.1 = (bf16[2,64,1024]{2,1,0:T(8,128)(2,1)S(1)}, bf16[2,64,1024]{2,1,0:T(8,128)(2,1)S(1)}, u32[]{:S(2)}, u32[]{:S(2)}) collective-permute-start(bf16[2,64,1024]{2,1,0:T(8,128)(2,1)S(1)} %shard_map.86.rest_0_), channel_id=1, source_target_pairs={{0,1},{1,2},{2,3},{3,4},{4,5},{5,6},{6,7},{7,0},{8,9},{9,10},{10,1... | collective-permute-start | bytes 786440 | tf_op jit(solution)/shard_map/ppermute | solution.py:27
  12.6 15.9 %collective-permute-start = (bf16[2,64,1024]{2,1,0:T(8,128)(2,1)S(1)}, bf16[2,64,1024]{2,1,0:T(8,128)(2,1)S(1)}, u32[]{:S(2)}, u32[]{:S(2)}) collective-permute-start(bf16[2,64,1024]{2,1,0:T(8,128)(2,1)S(1)} %shard_map.85.rest_0_), channel_id=1, source_target_pairs={{0,8},{8,16},{16,24},{24,32},{32,40},{40,48},{48,56},{56,64},{64,7... | collective-permute-start | bytes 786440 | tf_op jit(solution)/shard_map/ppermute | solution.py:27
  24.4 6.4 %copy-start.6 = (f32[2,32,1024]{2,1,0:T(8,128)S(1)}, f32[2,32,1024]{2,1,0:T(8,128)}, u32[]{:S(2)}) copy-start(f32[2,32,1024]{2,1,0:T(8,128)} %constant.41.clone.coarse) | copy-start | bytes 786436
  24.5 6.4 %copy-start.7 = (f32[2,32,1024]{2,1,0:T(8,128)S(1)}, f32[2,32,1024]{2,1,0:T(8,128)}, u32[]{:S(2)}) copy-start(f32[2,32,1024]{2,1,0:T(8,128)} %constant.42.clone.fine) | copy-start | bytes 786436
  24.5 7.4 %collective-permute-start.7 = (bf16[2,64,1024]{2,1,0:T(8,128)(2,1)S(1)}, bf16[2,64,1024]{2,1,0:T(8,128)(2,1)S(1)}, u32[]{:S(2)}, u32[]{:S(2)}) collective-permute-start(bf16[2,64,1024]{2,1,0:T(8,128)(2,1)S(1)} %shard_map.88.rest_0_), channel_id=1, source_target_pairs={{0,1},{1,2},{2,3},{3,4},{4,5},{5,6},{6,7},{7,0},{8,9},{9,10},{10,1... | collective-permute-start | bytes 786440 | tf_op jit(solution)/shard_map/ppermute | solution.py:27
  26.3 12.5 %collective-permute-start.6 = (bf16[2,64,1024]{2,1,0:T(8,128)(2,1)S(1)}, bf16[2,64,1024]{2,1,0:T(8,128)(2,1)S(1)}, u32[]{:S(2)}, u32[]{:S(2)}) collective-permute-start(bf16[2,64,1024]{2,1,0:T(8,128)(2,1)S(1)} %get-tuple-element.22.rest_0_), channel_id=1, source_target_pairs={{0,8},{8,16},{16,24},{24,32},{32,40},{40,48},{48,56},{56,64},{64,7... | collective-permute-start | bytes 786440 | tf_op jit(solution)/shard_map/ppermute | solution.py:27
  29.3 14.2 %collective-permute-start.4 = (bf16[2,64,1024]{2,1,0:T(8,128)(2,1)S(1)}, bf16[2,64,1024]{2,1,0:T(8,128)(2,1)S(1)}, u32[]{:S(2)}, u32[]{:S(2)}) collective-permute-start(bf16[2,64,1024]{2,1,0:T(8,128)(2,1)S(1)} %get-tuple-element.23.rest_0_), channel_id=1, source_target_pairs={{0,8},{8,16},{16,24},{24,32},{32,40},{40,48},{48,56},{56,64},{64,7... | collective-permute-start | bytes 786440 | tf_op jit(solution)/shard_map/ppermute | solution.py:27
  30.2 10.4 %collective-permute-start.5 = (bf16[2,64,1024]{2,1,0:T(8,128)(2,1)S(1)}, bf16[2,64,1024]{2,1,0:T(8,128)(2,1)S(1)}, u32[]{:S(2)}, u32[]{:S(2)}) collective-permute-start(bf16[2,64,1024]{2,1,0:T(8,128)(2,1)S(1)} %shard_map.90._), channel_id=1, source_target_pairs={{0,1},{1,2},{2,3},{3,4},{4,5},{5,6},{6,7},{7,0},{8,9},{9,10},{10,1... | collective-permute-start | bytes 786440 | tf_op jit(solution)/shard_map/ppermute | solution.py:27
  40.3 5.8 %collective-permute-start.11 = (bf16[2,64,1024]{2,1,0:T(8,128)(2,1)S(1)}, bf16[2,64,1024]{2,1,0:T(8,128)(2,1)S(1)}, u32[]{:S(2)}, u32[]{:S(2)}) collective-permute-start(bf16[2,64,1024]{2,1,0:T(8,128)(2,1)S(1)} %shard_map.93.rest_1_), channel_id=1, source_target_pairs={{0,1},{1,2},{2,3},{3,4},{4,5},{5,6},{6,7},{7,0},{8,9},{9,10},{10,1... | collective-permute-start | bytes 786440 | tf_op jit(solution)/shard_map/ppermute | solution.py:27
  40.3 12.7 %collective-permute-start.10 = (bf16[2,64,1024]{2,1,0:T(8,128)(2,1)S(1)}, bf16[2,64,1024]{2,1,0:T(8,128)(2,1)S(1)}, u32[]{:S(2)}, u32[]{:S(2)}) collective-permute-start(bf16[2,64,1024]{2,1,0:T(8,128)(2,1)S(1)} %get-tuple-element.26.rest_1_), channel_id=1, source_target_pairs={{0,8},{8,16},{16,24},{24,32},{32,40},{40,48},{48,56},{56,64},{64,7... | collective-permute-start | bytes 786440 | tf_op jit(solution)/shard_map/ppermute | solution.py:27
  45.1 10.1 %collective-permute-start.9 = (bf16[2,64,1024]{2,1,0:T(8,128)(2,1)S(1)}, bf16[2,64,1024]{2,1,0:T(8,128)(2,1)S(1)}, u32[]{:S(2)}, u32[]{:S(2)}) collective-permute-start(bf16[2,64,1024]{2,1,0:T(8,128)(2,1)S(1)} %shard_map.95.rest_1_), channel_id=1, source_target_pairs={{0,1},{1,2},{2,3},{3,4},{4,5},{5,6},{6,7},{7,0},{8,9},{9,10},{10,1... | collective-permute-start | bytes 786440 | tf_op jit(solution)/shard_map/ppermute | solution.py:27
  45.1 13.5 %collective-permute-start.8 = (bf16[2,64,1024]{2,1,0:T(8,128)(2,1)S(1)}, bf16[2,64,1024]{2,1,0:T(8,128)(2,1)S(1)}, u32[]{:S(2)}, u32[]{:S(2)}) collective-permute-start(bf16[2,64,1024]{2,1,0:T(8,128)(2,1)S(1)} %get-tuple-element.27.rest_1_), channel_id=1, source_target_pairs={{0,8},{8,16},{16,24},{24,32},{32,40},{40,48},{48,56},{56,64},{64,7... | collective-permute-start | bytes 786440 | tf_op jit(solution)/shard_map/ppermute | solution.py:27
  54.5 5.6 %collective-permute-start.18 = (bf16[2,64,1024]{2,1,0:T(8,128)(2,1)S(1)}, bf16[2,64,1024]{2,1,0:T(8,128)(2,1)S(1)}, u32[]{:S(2)}, u32[]{:S(2)}) collective-permute-start(bf16[2,64,1024]{2,1,0:T(8,128)(2,1)S(1)} %shard_map.97.rest_1_), channel_id=1, source_target_pairs={{0,7},{1,0},{2,1},{3,2},{4,3},{5,4},{6,5},{7,6},{8,15},{9,8},{10,9... | collective-permute-start | bytes 786440 | tf_op jit(solution)/shard_map/ppermute | solution.py:27
  55.2 5.8 %collective-permute-start.19 = (bf16[2,64,1024]{2,1,0:T(8,128)(2,1)S(1)}, bf16[2,64,1024]{2,1,0:T(8,128)(2,1)S(1)}, u32[]{:S(2)}, u32[]{:S(2)}) collective-permute-start(bf16[2,64,1024]{2,1,0:T(8,128)(2,1)S(1)} %shard_map.97.rest_1_), channel_id=1, source_target_pairs={{0,1},{1,2},{2,3},{3,4},{4,5},{5,6},{6,7},{7,0},{8,9},{9,10},{10,1... | collective-permute-start | bytes 786440 | tf_op jit(solution)/shard_map/ppermute | solution.py:27
  55.2 8.8 %collective-permute-start.16 = (bf16[2,64,1024]{2,1,0:T(8,128)(2,1)S(1)}, bf16[2,64,1024]{2,1,0:T(8,128)(2,1)S(1)}, u32[]{:S(2)}, u32[]{:S(2)}) collective-permute-start(bf16[2,64,1024]{2,1,0:T(8,128)(2,1)S(1)} %get-tuple-element.30.rest_2_), channel_id=1, source_target_pairs={{0,8},{8,0},{16,24},{24,16},{32,40},{40,32},{48,56},{56,48},{64,72... | collective-permute-start | bytes 786440 | tf_op jit(solution)/shard_map/ppermute | solution.py:34
  55.2 9.5 %collective-permute-start.17 = (bf16[2,64,1024]{2,1,0:T(8,128)(2,1)S(1)}, bf16[2,64,1024]{2,1,0:T(8,128)(2,1)S(1)}, u32[]{:S(2)}, u32[]{:S(2)}) collective-permute-start(bf16[2,64,1024]{2,1,0:T(8,128)(2,1)S(1)} %get-tuple-element.30.rest_2_), channel_id=1, source_target_pairs={{0,0},{8,16},{16,8},{24,32},{32,24},{40,48},{48,40},{56,64},{64,56... | collective-permute-start | bytes 786440 | tf_op jit(solution)/shard_map/ppermute | solution.py:34
  60.1 6.2 %collective-permute-start.14 = (bf16[2,64,1024]{2,1,0:T(8,128)(2,1)S(1)}, bf16[2,64,1024]{2,1,0:T(8,128)(2,1)S(1)}, u32[]{:S(2)}, u32[]{:S(2)}) collective-permute-start(bf16[2,64,1024]{2,1,0:T(8,128)(2,1)S(1)} %shard_map.99.held), channel_id=1, source_target_pairs={{0,7},{1,0},{2,1},{3,2},{4,3},{5,4},{6,5},{7,6},{8,15},{9,8},{10,9... | collective-permute-start | bytes 786440 | tf_op jit(solution)/shard_map/ppermute | solution.py:27
  60.1 6.2 %collective-permute-start.15 = (bf16[2,64,1024]{2,1,0:T(8,128)(2,1)S(1)}, bf16[2,64,1024]{2,1,0:T(8,128)(2,1)S(1)}, u32[]{:S(2)}, u32[]{:S(2)}) collective-permute-start(bf16[2,64,1024]{2,1,0:T(8,128)(2,1)S(1)} %shard_map.99.held), channel_id=1, source_target_pairs={{0,1},{1,2},{2,3},{3,4},{4,5},{5,6},{6,7},{7,0},{8,9},{9,10},{10,1... | collective-permute-start | bytes 786440 | tf_op jit(solution)/shard_map/ppermute | solution.py:27
  61.0 9.1 %collective-permute-start.12 = (bf16[2,64,1024]{2,1,0:T(8,128)(2,1)S(1)}, bf16[2,64,1024]{2,1,0:T(8,128)(2,1)S(1)}, u32[]{:S(2)}, u32[]{:S(2)}) collective-permute-start(bf16[2,64,1024]{2,1,0:T(8,128)(2,1)S(1)} %get-tuple-element.31.rest_2_), channel_id=1, source_target_pairs={{0,8},{8,0},{16,24},{24,16},{32,40},{40,32},{48,56},{56,48},{64,72... | collective-permute-start | bytes 786440 | tf_op jit(solution)/shard_map/ppermute | solution.py:34
  64.0 6.1 %collective-permute-start.13 = (bf16[2,64,1024]{2,1,0:T(8,128)(2,1)S(1)}, bf16[2,64,1024]{2,1,0:T(8,128)(2,1)S(1)}, u32[]{:S(2)}, u32[]{:S(2)}) collective-permute-start(bf16[2,64,1024]{2,1,0:T(8,128)(2,1)S(1)} %get-tuple-element.31.rest_2_), channel_id=1, source_target_pairs={{0,0},{8,16},{16,8},{24,32},{32,24},{40,48},{48,40},{56,64},{64,56... | collective-permute-start | bytes 786440 | tf_op jit(solution)/shard_map/ppermute | solution.py:34
  66.3 36.1 %copy-start.8 = (bf16[256,256]{1,0:T(8,128)(2,1)S(1)}, bf16[256,256]{1,0:T(8,128)(2,1)}, u32[]{:S(2)}) copy-start(bf16[256,256]{1,0:T(8,128)(2,1)} %constant.43.clone.weights) | copy-start | bytes 393220
  66.3 36.1 %copy-start.9 = (f32[256,1]{1,0:T(8,128)S(1)}, f32[256,1]{1,0:T(8,128)}, u32[]{:S(2)}) copy-start(f32[256,1]{1,0:T(8,128)} %constant.44.clone.gain) | copy-start | bytes 3076
